TPU v7x, 32 devices: a whole 2x2x4 slice. The times are simulated.
32 devices in a mesh: dp: 4 (over y, core), ctx: 8 (over z, x).
Axes of the slice: x: 2, y: 2, z: 4, core: 2. Of those that a mesh axis runs over, the one named last changes fastest.
Arguments:
- tokens: bfloat16 [2, 4, 1024, 768], P(None, 'dp', 'ctx'), may hold values from -6 to 6
- lengths: int32 [2, 4], P(None, 'dp'), may hold values from 513 to 1024, as said below
- routes: int32 [2, 4, 1024, 2], P(None, 'dp', 'ctx'), may hold values from 0 to 3, all different within a row
- cotangent: bfloat16 [2, 4, 1024, 768], P(None, 'dp', 'ctx'), may hold values from -6 to 6
- attn_gain: bfloat16 [768], P(('dp', 'ctx')), may hold values from 0.5 to 1.5
- attn_in: bfloat16 [768, 2304], P(('dp', 'ctx')), may hold values from -0.21875 to 0.21875
- attn_out: bfloat16 [768, 768], P(('dp', 'ctx')), may hold values from -3.5 to 3.5
- ffn_gain: bfloat16 [768], P(('dp', 'ctx')), may hold values from 0.5 to 1.5
- router: bfloat16 [768, 4], P(('dp', 'ctx')), may hold values from -0.21875 to 0.21875
- dense_in: bfloat16 [768, 4096], P(('dp', 'ctx')), may hold values from -0.21875 to 0.21875
- dense_out: bfloat16 [2048, 768], P(('dp', 'ctx')), may hold values from -0.125 to 0.125
- expert_in: bfloat16 [768, 4, 4096], P(('dp', 'ctx')), may hold values from -0.21875 to 0.21875
- expert_out: bfloat16 [2048, 4, 768], P(('dp', 'ctx')), may hold values from -0.125 to 0.125
Outputs:
- activations: bfloat16 [2, 4, 1024, 768], P(None, 'dp', 'ctx')
- input_grad: bfloat16 [2, 4, 1024, 768], P(None, 'dp', 'ctx')
- attn_gain_grad: float32 [768], P(('dp', 'ctx'))
- attn_in_grad: float32 [768, 2304], P(('dp', 'ctx'))
- attn_out_grad: float32 [768, 768], P(('dp', 'ctx'))
- ffn_gain_grad: float32 [768], P(('dp', 'ctx'))
- router_grad: float32 [768, 4], P(('dp', 'ctx'))
- dense_in_grad: float32 [768, 4096], P(('dp', 'ctx'))
- dense_out_grad: float32 [2048, 768], P(('dp', 'ctx'))
- expert_in_grad: float32 [768, 4, 4096], P(('dp', 'ctx'))
- expert_out_grad: float32 [2048, 4, 768], P(('dp', 'ctx'))
Inputs may be any that keep to these rules, and one draw needn't show every extreme that they name: `lengths`: the first sequence of every micro-batch is valid in all 1024 slots. `routes`: each slot names two different experts.
All inputs are finite; a program needn't handle non-finite values.
Results may differ from a plain program's by a relative error of at most 0.014.
Values may be sent and summed in bfloat16 or wider, within the bound.
A program may use at most 384 MiB of HBM per device.

v0:
```python
import jax
import jax.numpy as jnp
from jax import lax
from jax.sharding import PartitionSpec as P

HEADS = 12
HEAD_DIM = 64
FF = 2048


epsilon = 1e-05


def rotate(values, places, direction_sign):
    half_dim = values.shape[-1] // 2
    frequency = 10000.0 ** (-jnp.arange(half_dim, dtype=jnp.float32) / half_dim)
    angles = places.astype(jnp.float32)[:, None] * frequency[None, :]
    cosine = jnp.cos(angles)[:, None, :]
    sine_part = direction_sign * jnp.sin(angles)[:, None, :]
    leading = values[..., :half_dim]
    trailing = values[..., half_dim:]
    return jnp.concatenate(
        [leading * cosine - trailing * sine_part, trailing * cosine + leading * sine_part], axis=-1
    )


def norm_forward(row_data, gain_row):
    inverse = lax.rsqrt(jnp.mean(row_data * row_data, axis=-1, keepdims=True) + epsilon)
    return ((row_data * inverse * gain_row.astype(jnp.float32)).astype(jnp.bfloat16), inverse)


def norm_backward(row_data, inverse, gain_row, gradient):
    scaled = gradient * gain_row.astype(jnp.float32)
    gain_grad = jnp.sum(gradient * row_data * inverse, axis=(0, 1))
    row_grad = inverse * scaled - row_data * inverse**3 * jnp.mean(
        scaled * row_data, axis=-1, keepdims=True
    )
    return (row_grad, gain_grad)


def swiglu_forward(normed, weight_in, weight_out):
    pre_act = jnp.einsum("scd,df->scf", normed, weight_in, preferred_element_type=jnp.float32)
    activated = (jax.nn.silu(pre_act[..., :FF]) * pre_act[..., FF:]).astype(jnp.bfloat16)
    branch = jnp.einsum("scf,fd->scd", activated, weight_out, preferred_element_type=jnp.float32)
    return (pre_act, activated, branch)


def swiglu_backward(normed, weight_in, weight_out, pre_act, activated, out_grad):
    weight_out_grad = jnp.einsum(
        "scf,scd->fd", activated, out_grad, preferred_element_type=jnp.float32
    )
    act_grad = jnp.einsum("scd,fd->scf", out_grad, weight_out, preferred_element_type=jnp.float32)
    gate_part = pre_act[..., :FF]
    up_part = pre_act[..., FF:]
    sigmoid_gate = jax.nn.sigmoid(gate_part)
    gate_grad = act_grad * up_part * sigmoid_gate * (1.0 + gate_part * (1.0 - sigmoid_gate))
    up_grad = act_grad * gate_part * sigmoid_gate
    pre_grad = jnp.concatenate([gate_grad, up_grad], axis=-1).astype(jnp.bfloat16)
    weight_in_grad = jnp.einsum("scd,scf->df", normed, pre_grad, preferred_element_type=jnp.float32)
    normed_grad = jnp.einsum("scf,df->scd", pre_grad, weight_in, preferred_element_type=jnp.float32)
    return (weight_in_grad, weight_out_grad, normed_grad)


def head_scores(query_head, key_head, query_places, key_places, seq_lengths):
    raw_scores = (
        jnp.einsum("sqd,skd->sqk", query_head, key_head, preferred_element_type=jnp.float32) * 0.125
    )
    allowed = (key_places[None, None, :] <= query_places[None, :, None]) & (
        key_places[None, None, :] < seq_lengths[:, None, None]
    )
    return jnp.where(allowed, raw_scores, -1000000000.0)


def heads_first(rows, seq_count):
    split_rows = rows.reshape(seq_count, rows.shape[1], HEADS, HEAD_DIM)
    return jnp.moveaxis(split_rows, 2, 0)


def heads_back(stacked, seq_count):
    return jnp.moveaxis(stacked, 0, 2).reshape(seq_count, stacked.shape[2], HEADS * HEAD_DIM)


def shards(
    tokens,
    lengths,
    routes,
    cotangent,
    attn_gain,
    attn_in,
    attn_out,
    ffn_gain,
    router,
    dense_in,
    dense_out,
    expert_in,
    expert_out,
):
    micro_count, seq_count, block_len, model_width = tokens.shape
    expert_count = expert_in.shape[1]
    ctx_count = lax.axis_size("ctx")
    query_places = lax.axis_index("ctx") * block_len + jnp.arange(block_len, dtype=jnp.int32)
    key_places = jnp.arange(block_len * ctx_count, dtype=jnp.int32)
    head_shape = (seq_count, block_len, HEADS, HEAD_DIM)
    expert_ids = jnp.arange(expert_count, dtype=jnp.int32)
    full_shapes = (
        (model_width,),
        (model_width, 3 * model_width),
        (model_width, model_width),
        (model_width,),
        (model_width, expert_count),
        (model_width, 2 * FF),
        (FF, model_width),
        (model_width, expert_count, 2 * FF),
        (FF, expert_count, model_width),
    )
    running = [jnp.zeros(shape_one, jnp.float32) for shape_one in full_shapes]
    owned_total = None
    output_rows = []
    input_rows = []
    for batch_index in range(micro_count):
        gathered = (
            lax.all_gather(attn_gain, ("dp", "ctx"), axis=0, tiled=True),
            lax.all_gather(attn_in, ("dp", "ctx"), axis=0, tiled=True),
            lax.all_gather(attn_out, ("dp", "ctx"), axis=0, tiled=True),
            lax.all_gather(ffn_gain, ("dp", "ctx"), axis=0, tiled=True),
            lax.all_gather(router, ("dp", "ctx"), axis=0, tiled=True),
            lax.all_gather(dense_in, ("dp", "ctx"), axis=0, tiled=True),
            lax.all_gather(dense_out, ("dp", "ctx"), axis=0, tiled=True),
            lax.all_gather(expert_in, ("dp", "ctx"), axis=0, tiled=True),
            lax.all_gather(expert_out, ("dp", "ctx"), axis=0, tiled=True),
        )
        (
            gain_one,
            weight_qkv,
            weight_mix,
            gain_two,
            weight_route,
            dense_up,
            dense_down,
            experts_up,
            experts_down,
        ) = gathered
        inputs = tokens[batch_index].astype(jnp.float32)
        seq_lengths = lengths[batch_index]
        normed, inverse_one = norm_forward(inputs, gain_one)
        projected = jnp.einsum(
            "scd,de->sce", normed, weight_qkv, preferred_element_type=jnp.float32
        )
        queries = rotate(
            projected[..., :model_width].reshape(head_shape), query_places, 1.0
        ).astype(jnp.bfloat16)
        key_rows = rotate(
            projected[..., model_width : 2 * model_width].reshape(head_shape), query_places, 1.0
        )
        key_rows = key_rows.astype(jnp.bfloat16).reshape(seq_count, block_len, model_width)
        value_rows = projected[..., 2 * model_width :].astype(jnp.bfloat16)
        key_all, value_all = (
            lax.all_gather(key_rows, "ctx", axis=1, tiled=True),
            lax.all_gather(value_rows, "ctx", axis=1, tiled=True),
        )
        query_stack = jnp.moveaxis(queries, 2, 0)

        def head_forward(packed):
            query_head, key_head, value_head = packed
            scores = head_scores(query_head, key_head, query_places, key_places, seq_lengths)
            row_max = jnp.max(scores, axis=-1, keepdims=True)
            log_head = row_max + jnp.log(jnp.sum(jnp.exp(scores - row_max), axis=-1, keepdims=True))
            probs_low = jnp.exp(scores - log_head).astype(jnp.bfloat16)
            attended_head = jnp.einsum(
                "sqk,skd->sqd", probs_low, value_head, preferred_element_type=jnp.float32
            )
            return (attended_head, log_head)

        attended_stack, log_total = lax.map(
            head_forward,
            (query_stack, heads_first(key_all, seq_count), heads_first(value_all, seq_count)),
        )
        attended = heads_back(attended_stack, seq_count).astype(jnp.bfloat16)
        middle = inputs + jnp.einsum(
            "scd,de->sce", attended, weight_mix, preferred_element_type=jnp.float32
        )
        normed_two, inverse_two = norm_forward(middle, gain_two)
        logits = jnp.einsum(
            "scd,de->sce", normed_two, weight_route, preferred_element_type=jnp.float32
        )
        choose = (routes[batch_index][..., None] == expert_ids).astype(jnp.float32)
        picked = jnp.sum(choose * logits[..., None, :], axis=-1)
        gate_probs = jax.nn.softmax(picked, axis=-1)
        mixing = jnp.sum(gate_probs[..., None] * choose, axis=-2)
        dense_saved = swiglu_forward(normed_two, dense_up, dense_down)
        expert_saved = [
            swiglu_forward(normed_two, experts_up[:, expert], experts_down[:, expert])
            for expert in range(expert_count)
        ]
        expert_sum = mixing[..., 0:1] * expert_saved[0][2]
        for expert in range(1, expert_count):
            expert_sum = expert_sum + mixing[..., expert : expert + 1] * expert_saved[expert][2]
        output_rows.append((middle + dense_saved[2] + expert_sum).astype(jnp.bfloat16))
        gathered_back = (
            lax.all_gather(attn_gain, ("dp", "ctx"), axis=0, tiled=True),
            lax.all_gather(attn_in, ("dp", "ctx"), axis=0, tiled=True),
            lax.all_gather(attn_out, ("dp", "ctx"), axis=0, tiled=True),
            lax.all_gather(ffn_gain, ("dp", "ctx"), axis=0, tiled=True),
            lax.all_gather(router, ("dp", "ctx"), axis=0, tiled=True),
            lax.all_gather(dense_in, ("dp", "ctx"), axis=0, tiled=True),
            lax.all_gather(dense_out, ("dp", "ctx"), axis=0, tiled=True),
            lax.all_gather(expert_in, ("dp", "ctx"), axis=0, tiled=True),
            lax.all_gather(expert_out, ("dp", "ctx"), axis=0, tiled=True),
        )
        key_back, value_back = (
            lax.all_gather(key_rows, "ctx", axis=1, tiled=True),
            lax.all_gather(value_rows, "ctx", axis=1, tiled=True),
        )
        (
            gain_one,
            weight_qkv,
            weight_mix,
            gain_two,
            weight_route,
            dense_up,
            dense_down,
            experts_up,
            experts_down,
        ) = gathered_back
        valid_rows = (query_places[None, :] < seq_lengths[:, None]).astype(jnp.float32)
        grad_rows = cotangent[batch_index].astype(jnp.float32) * valid_rows[..., None]
        dense_in_part, dense_out_part, normed_two_grad = swiglu_backward(
            normed_two,
            dense_up,
            dense_down,
            dense_saved[0],
            dense_saved[1],
            grad_rows.astype(jnp.bfloat16),
        )
        running[5] = running[5] + dense_in_part
        running[6] = running[6] + dense_out_part
        mixing_parts = []
        for expert in range(expert_count):
            mixing_parts.append(jnp.sum(grad_rows * expert_saved[expert][2], axis=-1))
            out_expert = (mixing[..., expert : expert + 1] * grad_rows).astype(jnp.bfloat16)
            in_part, out_part, normed_part = swiglu_backward(
                normed_two,
                experts_up[:, expert],
                experts_down[:, expert],
                expert_saved[expert][0],
                expert_saved[expert][1],
                out_expert,
            )
            running[7] = running[7].at[:, expert].add(in_part)
            running[8] = running[8].at[:, expert].add(out_part)
            normed_two_grad = normed_two_grad + normed_part
        mixing_grad = jnp.stack(mixing_parts, axis=-1)
        choice_grad = jnp.sum(choose * mixing_grad[..., None, :], axis=-1)
        pick_grad = gate_probs * (
            choice_grad - jnp.sum(gate_probs * choice_grad, axis=-1, keepdims=True)
        )
        logit_grad = jnp.sum(pick_grad[..., None] * choose, axis=-2).astype(jnp.bfloat16)
        running[4] = running[4] + jnp.einsum(
            "scd,sce->de", normed_two, logit_grad, preferred_element_type=jnp.float32
        )
        normed_two_grad = normed_two_grad + jnp.einsum(
            "sce,de->scd", logit_grad, weight_route, preferred_element_type=jnp.float32
        )
        middle_part, gain_two_grad = norm_backward(middle, inverse_two, gain_two, normed_two_grad)
        running[3] = running[3] + gain_two_grad
        middle_grad = grad_rows + middle_part
        attn_low = middle_grad.astype(jnp.bfloat16)
        running[2] = running[2] + jnp.einsum(
            "scd,sce->de", attended, attn_low, preferred_element_type=jnp.float32
        )
        attended_grad = jnp.einsum(
            "sce,de->scd", attn_low, weight_mix, preferred_element_type=jnp.float32
        )
        attended_grad = attended_grad.astype(jnp.bfloat16)

        def head_backward(packed):
            query_head, key_head, value_head, upstream, log_head = packed
            scores = head_scores(query_head, key_head, query_places, key_places, seq_lengths)
            probs_full = jnp.exp(scores - log_head)
            probs_low = probs_full.astype(jnp.bfloat16)
            value_grad_head = jnp.einsum(
                "sqk,sqd->skd", probs_low, upstream, preferred_element_type=jnp.float32
            )
            prob_grad = jnp.einsum(
                "sqd,skd->sqk", upstream, value_head, preferred_element_type=jnp.float32
            )
            score_grad = probs_full * (
                prob_grad - jnp.sum(probs_full * prob_grad, axis=-1, keepdims=True)
            )
            score_grad = score_grad.astype(jnp.bfloat16)
            query_grad_head = (
                jnp.einsum("sqk,skd->sqd", score_grad, key_head, preferred_element_type=jnp.float32)
                * 0.125
            )
            key_grad_head = (
                jnp.einsum(
                    "sqk,sqd->skd", score_grad, query_head, preferred_element_type=jnp.float32
                )
                * 0.125
            )
            return (query_grad_head, key_grad_head, value_grad_head)

        query_grad_stack, key_grad_stack, value_grad_stack = lax.map(
            head_backward,
            (
                query_stack,
                heads_first(key_back, seq_count),
                heads_first(value_back, seq_count),
                heads_first(attended_grad, seq_count),
                log_total,
            ),
        )
        key_grad, value_grad = (
            lax.psum_scatter(
                heads_back(key_grad_stack, seq_count), "ctx", scatter_dimension=1, tiled=True
            ),
            lax.psum_scatter(
                heads_back(value_grad_stack, seq_count), "ctx", scatter_dimension=1, tiled=True
            ),
        )
        query_grad = jnp.moveaxis(query_grad_stack, 0, 2)
        projected_grad = jnp.concatenate(
            [
                rotate(query_grad, query_places, -1.0).reshape(seq_count, block_len, model_width),
                rotate(key_grad.reshape(head_shape), query_places, -1.0).reshape(
                    seq_count, block_len, model_width
                ),
                value_grad,
            ],
            axis=-1,
        ).astype(jnp.bfloat16)
        running[1] = running[1] + jnp.einsum(
            "scd,sce->de", normed, projected_grad, preferred_element_type=jnp.float32
        )
        normed_grad = jnp.einsum(
            "sce,de->scd", projected_grad, weight_qkv, preferred_element_type=jnp.float32
        )
        input_part, gain_one_grad = norm_backward(inputs, inverse_one, gain_one, normed_grad)
        running[0] = running[0] + gain_one_grad
        input_rows.append((middle_grad + input_part).astype(jnp.bfloat16))
    owned_total = (
        lax.psum_scatter(running[0], ("dp", "ctx"), scatter_dimension=0, tiled=True),
        lax.psum_scatter(running[1], ("dp", "ctx"), scatter_dimension=0, tiled=True),
        lax.psum_scatter(running[2], ("dp", "ctx"), scatter_dimension=0, tiled=True),
        lax.psum_scatter(running[3], ("dp", "ctx"), scatter_dimension=0, tiled=True),
        lax.psum_scatter(running[4], ("dp", "ctx"), scatter_dimension=0, tiled=True),
        lax.psum_scatter(running[5], ("dp", "ctx"), scatter_dimension=0, tiled=True),
        lax.psum_scatter(running[6], ("dp", "ctx"), scatter_dimension=0, tiled=True),
        lax.psum_scatter(running[7], ("dp", "ctx"), scatter_dimension=0, tiled=True),
        lax.psum_scatter(running[8], ("dp", "ctx"), scatter_dimension=0, tiled=True),
    )
    return (
        jnp.stack(output_rows),
        jnp.stack(input_rows),
        owned_total[0],
        owned_total[1],
        owned_total[2],
        owned_total[3],
        owned_total[4],
        owned_total[5],
        owned_total[6],
        owned_total[7],
        owned_total[8],
    )


def solution(mesh):
    in_specs = (
        P(None, "dp", "ctx", None),
        P(None, "dp"),
        P(None, "dp", "ctx", None),
        P(None, "dp", "ctx", None),
        P(("dp", "ctx")),
        P(("dp", "ctx"), None),
        P(("dp", "ctx"), None),
        P(("dp", "ctx")),
        P(("dp", "ctx"), None),
        P(("dp", "ctx"), None),
        P(("dp", "ctx"), None),
        P(("dp", "ctx"), None, None),
        P(("dp", "ctx"), None, None),
    )
    out_specs = (
        P(None, "dp", "ctx", None),
        P(None, "dp", "ctx", None),
        P(("dp", "ctx")),
        P(("dp", "ctx"), None),
        P(("dp", "ctx"), None),
        P(("dp", "ctx")),
        P(("dp", "ctx"), None),
        P(("dp", "ctx"), None),
        P(("dp", "ctx"), None),
        P(("dp", "ctx"), None, None),
        P(("dp", "ctx"), None, None),
    )
    return jax.shard_map(shards, mesh=mesh, in_specs=in_specs, out_specs=out_specs, check_vma=False)
```

profile of v0, /device:TPU:0, one launch (start us, length us, event | category | flops | bytes accessed | tf_op | source)
XLA Modules:
  0.0 2421.5 jit_solution(13480178706031614726)
XLA Ops:
  9.7 42.3 %all-reduce.8 = (bf16[768]{0:T(1024)(128)(2,1)S(1)}, bf16[768]{0:T(1024)(128)(2,1)S(1)}) all-reduce(bf16[768]{0:T(1024)(128)(2,1)S(1)} %dynamic-update-slice.48, bf16[768]{0:T(1024)(128)(2,1)S(1)} %dynamic-update-slice.49), channel_id=1, replica_groups=mesh['dp'=4,'ctx'=8] {'dp','ctx'}, use_global_device_ids=true, to_apply=%add.2 | all-reduce | flops 1536 | bytes 6144
  54.4 19.6 all-gather.12.cloned.1.call-done
  98.9 66.5 %all-gather = bf16[32,24,4]{1,2,0:T(4,128)(2,1)S(1)} all-gather(bf16[1,24,4]{1,2,0:T(4,128)(2,1)S(1)} %bitcast.959), channel_id=1, replica_groups=mesh['dp'=4,'ctx'=8] {'dp','ctx'}, dimensions={0}, use_global_device_ids=true | all-gather | bytes 6336 | tf_op jit(solution)/shard_map/all_gather | solution.py:126
  181.6 40.3 %all-gather.16.cloned.1.call-done = bf16[1,1024,768]{2,1,0:T(8,128)(2,1)} async-done(((bf16[1,128,768]{2,1,0:T(8,128)(2,1)}), bf16[1,1024,768]{2,1,0:T(8,128)(2,1)}) %all-gather.16.cloned.1.call-update) | async-done | bytes 1572880 | tf_op jit(solution)/shard_map/all_gather | solution.py:159
  228.1 43.6 %while.76 = (s32[]{:T(128)}, bf16[12,1,128,64]{2,3,1,0:T(8,128)(2,1)}, f32[12,1,128,1]{2,3,1,0:T(1,128)}, s32[1,1]{1,0:T(1,128)}, bf16[12,1,128,64]{3,2,1,0:T(8,...) while((s32[]{:T(128)}, ...), condition=%wide.region_4.5_spmd.clone.clone, body=%wide.region_1.4_spmd.clone.clone.sunk | while | flops 34735104 | bytes 2172017 | solution.py:174
  281.1 42.6 %all-gather.30.cloned.1.call-done = bf16[1,1024,768]{2,1,0:T(8,128)(2,1)} async-done(((bf16[1,128,768]{2,1,0:T(8,128)(2,1)}), bf16[1,1024,768]{2,1,0:T(8,128)(2,1)}) %all-gather.30.cloned.1.call-update) | async-done | bytes 1572880 | tf_op jit(solution)/shard_map/all_gather | solution.py:159
  330.5 49.1 %while.77 = (s32[]{:T(128)}, bf16[12,1,128,64]{2,3,1,0:T(8,128)(2,1)}, f32[12,1,128,1]{2,3,1,0:T(1,128)S(1)}, s32[1,1]{1,0:T(1,128)}, bf16[12,1,128,64]{3,2,1,0:...) while((s32[]{:T(128)}, ...), condition=%wide.region_14.15_spmd.clone.clone, body=%wide.region_11.14_spmd.clone.clone.sunk | while | flops 34735104 | bytes 2172017 | solution.py:174
  381.5 13.7 all-gather.20.cloned.1.call-done
  402.9 52.9 %all-gather.22.cloned.1.call-done = bf16[2048,768]{1,0:T(8,128)(2,1)} async-done(((bf16[64,768]{1,0:T(8,128)(2,1)}), bf16[2048,768]{1,0:T(8,128)(2,1)}) %all-gather.22.cloned.1.call-update) | async-done | bytes 3145744 | tf_op jit(solution)/shard_map/all_gather | solution.py:128
  469.6 143.1 %all-gather.24.cloned.1.call-done = bf16[768,4,4096]{2,0,1:T(8,128)(2,1)} async-done(((bf16[24,4,4096]{2,0,1:T(8,128)(2,1)}), bf16[768,4,4096]{2,0,1:T(8,128)(2,1)}) %all-gather.24.cloned.1.call-update) | async-done | bytes 25165840 | tf_op jit(solution)/shard_map/all_gather | solution.py:129
  643.1 66.6 %all-gather.26.cloned.1.call-done = bf16[2048,4,768]{2,0,1:T(8,128)(2,1)} async-done(((bf16[64,4,768]{2,0,1:T(8,128)(2,1)}), bf16[2048,4,768]{2,0,1:T(8,128)(2,1)}) %all-gather.26.cloned.1.call-update) | async-done | bytes 12582928 | tf_op jit(solution)/shard_map/all_gather | solution.py:130
  793.8 93.5 %while.79 = (s32[]{:T(128)}, f32[12,1,128,64]{2,3,1,0:T(8,128)S(1)}, f32[12,1,1024,64]{2,3,1,0:T(8,128)}, f32[12,1,1024,64]{2,3,1,0:T(8,128)}, s32[1,1]{1,0:T(1,...) while((s32[]{:T(128)}, ...), condition=%wide.region_44.45_spmd.clone.clone, body=%wide.region_42.44_spmd.clone.clone.sunk | while | flops 85402624 | bytes 5384841 | solution.py:303
  891.5 94.0 %while.78 = (s32[]{:T(128)}, f32[12,1,128,64]{2,3,1,0:T(8,128)S(1)}, f32[12,1,1024,64]{2,3,1,0:T(8,128)}, f32[12,1,1024,64]{2,3,1,0:T(8,128)}, s32[1,1]{1,0:T(1,...) while((s32[]{:T(128)}, ...), condition=%wide.region_30.31_spmd.clone.clone, body=%wide.region_28.30_spmd.clone.clone.sunk | while | flops 85402624 | bytes 5384841 | solution.py:303
  990.9 13.3 scatter-add.66
  1014.6 6.6 fusion.112
  1027.7 6.7 fusion.110
  1041.0 6.7 fusion.108
  1050.8 16.4 scatter-add.54
  1073.7 11.1 fusion.107
  1084.8 11.2 fusion.106
  1096.1 11.2 fusion.105
  1107.3 11.1 fusion.104
  1118.4 11.3 fusion.103
  1129.7 11.1 fusion.102
  1162.6 51.3 %reduce-scatter.14.cloned.1.call-done = f32[1,128,768]{1,2,0:T(8,128)} async-done(((f32[1,1024,768]{1,2,0:T(8,128)}), f32[1,128,768]{1,2,0:T(8,128)}) %reduce-scatter.14.cloned.1.call-update) | async-done | bytes 393232 | tf_op jit(solution)/shard_map/reduce_scatter | solution.py:317
  1230.2 40.1 %all-reduce.7 = (f32[768]{0:T(1024)S(1)}, f32[768]{0:T(1024)S(1)}, f32[768,4]{0,1:T(4,128)S(1)}) all-reduce(f32[768]{0:T(1024)S(1)} %add.529, f32[768]{0:T(1024)S(1)} %add.532, f32[768,4]{0,1:T(4,128)S(1)} %convolution_add_fusion.10), channel_id=6, replica_groups=mesh['dp'=4,'ctx'=8] {'dp','ctx'}, use_global_device_ids=true, to_apply=%region_50.51.clone | all-reduce | flops 4608 | bytes 36864
  1273.2 191.9 %reduce-scatter.30.cloned.1.call-done = f32[64,4,768]{2,0,1:T(8,128)} async-done(((f32[2048,4,768]{2,0,1:T(8,128)}), f32[64,4,768]{2,0,1:T(8,128)}) %reduce-scatter.30.cloned.1.call-update) | async-done | bytes 786448 | tf_op jit(solution)/shard_map/reduce_scatter | solution.py:350
  1467.6 436.1 %reduce-scatter.28.cloned.1.call-done = f32[24,4,4096]{2,0,1:T(8,128)} async-done(((f32[768,4,4096]{2,0,1:T(8,128)}), f32[24,4,4096]{2,0,1:T(8,128)}) %reduce-scatter.28.cloned.1.call-update) | async-done | bytes 1572880 | tf_op jit(solution)/shard_map/reduce_scatter | solution.py:349
  1907.2 116.8 %reduce-scatter.26.cloned.1.call-done = f32[64,768]{1,0:T(8,128)} async-done(((f32[2048,768]{1,0:T(8,128)}), f32[64,768]{1,0:T(8,128)}) %reduce-scatter.26.cloned.1.call-update) | async-done | bytes 196624 | tf_op jit(solution)/shard_map/reduce_scatter | solution.py:348
  2024.0 161.1 %reduce-scatter.24.cloned.1.call-done = f32[24,4096]{1,0:T(8,128)} async-done(((f32[768,4096]{1,0:T(8,128)}), f32[24,4096]{1,0:T(8,128)}) %reduce-scatter.24.cloned.1.call-update) | async-done | bytes 393232 | tf_op jit(solution)/shard_map/reduce_scatter | solution.py:347
  2185.1 104.8 %reduce-scatter.22.cloned.1.call-done = f32[24,768]{1,0:T(8,128)} async-done(((f32[768,768]{1,0:T(8,128)}), f32[24,768]{1,0:T(8,128)}) %reduce-scatter.22.cloned.1.call-update) | async-done | bytes 73744 | tf_op jit(solution)/shard_map/reduce_scatter | solution.py:344
  2290.0 124.4 %reduce-scatter.20.cloned.1.call-done = f32[24,2304]{1,0:T(8,128)} async-done(((f32[768,2304]{1,0:T(8,128)}), f32[24,2304]{1,0:T(8,128)}) %reduce-scatter.20.cloned.1.call-update) | async-done | bytes 221200 | tf_op jit(solution)/shard_map/reduce_scatter | solution.py:343
  (931 shorter events, 572.3 us)
Async XLA Ops:
  7.2 66.9 %all-gather.12.cloned.1.call-start = ((), (), s32[]{:S(2)}) async-start(), calls=%async_computation.10 | async-start | bytes 3649536 | tf_op jit(solution)/shard_map/all_gather | solution.py:123
  7.9 161.4 %all-gather.28.cloned.1.call-start = ((), (), s32[]{:S(2)}) async-start(), calls=%async_computation.18 | async-start | bytes 1769472 | tf_op jit(solution)/shard_map/all_gather | solution.py:158
  87.5 89.9 %all-gather.14.cloned.1.call-start = ((), (), s32[]{:S(2)}) async-start(), calls=%async_computation.11 | async-start | bytes 1769472 | tf_op jit(solution)/shard_map/all_gather | solution.py:158
  88.3 133.6 %all-gather.16.cloned.1.call-start = ((), (), s32[]{:S(2)}) async-start(), calls=%async_computation.12 | async-start | bytes 1769472 | tf_op jit(solution)/shard_map/all_gather | solution.py:159
  90.1 187.9 %all-gather.18.cloned.1.call-start = ((), (), s32[]{:S(2)}) async-start(), calls=%async_computation.13 | async-start | bytes 1216512 | tf_op jit(solution)/shard_map/all_gather | solution.py:124
  90.7 233.0 %all-gather.30.cloned.1.call-start = ((), (), s32[]{:S(2)}) async-start(), calls=%async_computation.19 | async-start | bytes 1769472 | tf_op jit(solution)/shard_map/all_gather | solution.py:159
  92.4 302.8 %all-gather.20.cloned.1.call-start = ((), (), s32[]{:S(2)}) async-start(), calls=%async_computation.14 | async-start | bytes 6488064 | tf_op jit(solution)/shard_map/all_gather | solution.py:127
  93.2 362.6 %all-gather.22.cloned.1.call-start = ((), (), s32[]{:S(2)}) async-start(), calls=%async_computation.15 | async-start | bytes 3244032 | tf_op jit(solution)/shard_map/all_gather | solution.py:128
  93.9 518.8 %all-gather.24.cloned.1.call-start = ((), (), s32[]{:S(2)}) async-start(), calls=%async_computation.16 | async-start | bytes 25952256 | tf_op jit(solution)/shard_map/all_gather | solution.py:129
  95.3 614.5 %all-gather.26.cloned.1.call-start = ((), (), s32[]{:S(2)}) async-start(), calls=%async_computation.17 | async-start | bytes 12976128 | tf_op jit(solution)/shard_map/all_gather | solution.py:130
  96.2 1063.4 %reduce-scatter.16.cloned.1.call-start = ((), (), s32[]{:S(2)}) async-start(), calls=%async_computation.22 | async-start | bytes 3538944 | tf_op jit(solution)/shard_map/reduce_scatter | solution.py:314
  271.8 58.7 %copy-start.11 = (bf16[12,1,1024,64]{3,2,1,0:T(8,128)(2,1)}, bf16[12,1,1024,64]{3,2,1,0:T(8,128)(2,1)S(1)}, u32[]{:S(2)}) copy-start(bf16[12,1,1024,64]{3,2,1,0:T(8,128)(2,1)S(1)} %get-tuple-element.1489) | copy-start | bytes 4718596
  381.0 404.3 %copy-start.17 = (f32[128,768]{1,0:T(8,128)}, f32[128,768]{1,0:T(8,128)S(1)}, u32[]{:S(2)}) copy-start(f32[128,768]{1,0:T(8,128)S(1)} %get-tuple-element.1056) | copy-start | bytes 1179652
  381.2 258.5 %copy-start.3 = (bf16[128,768]{1,0:T(8,128)(2,1)}, bf16[128,768]{1,0:T(8,128)(2,1)S(1)}, u32[]{:S(2)}) copy-start(bf16[128,768]{1,0:T(8,128)(2,1)S(1)} %get-tuple-element.1029) | copy-start | bytes 589828
  728.4 55.8 %copy-start.142 = (bf16[128,4]{0,1:T(4,128)(2,1)}, bf16[128,4]{0,1:T(4,128)(2,1)S(1)}, u32[]{:S(2)}) copy-start(bf16[128,4]{0,1:T(4,128)(2,1)S(1)} %get-tuple-element.861) | copy-start | bytes 3076
  728.5 258.8 %copy-start.154 = (f32[128]{0:T(128)}, f32[128]{0:T(128)S(1)}, u32[]{:S(2)}) copy-start(f32[128]{0:T(128)S(1)} %get-tuple-element.1030) | copy-start | bytes 1540
  728.5 275.8 %copy-start.155 = (f32[128]{0:T(128)}, f32[128]{0:T(128)S(1)}, u32[]{:S(2)}) copy-start(f32[128]{0:T(128)S(1)} %get-tuple-element.1033) | copy-start | bytes 1540
  728.5 279.5 %copy-start.157 = (f32[128]{0:T(128)}, f32[128]{0:T(128)S(1)}, u32[]{:S(2)}) copy-start(f32[128]{0:T(128)S(1)} %get-tuple-element.1032) | copy-start | bytes 1540
  728.5 286.1 %copy-start.156 = (f32[128]{0:T(128)}, f32[128]{0:T(128)S(1)}, u32[]{:S(2)}) copy-start(f32[128]{0:T(128)S(1)} %get-tuple-element.1031) | copy-start | bytes 1540
  728.7 292.5 %copy-start.158 = (f32[128]{0:T(128)}, f32[128]{0:T(128)S(1)}, u32[]{:S(2)}) copy-start(f32[128]{0:T(128)S(1)} %get-tuple-element.1036) | copy-start | bytes 1540
  728.7 299.0 %copy-start.161 = (f32[128]{0:T(128)}, f32[128]{0:T(128)S(1)}, u32[]{:S(2)}) copy-start(f32[128]{0:T(128)S(1)} %get-tuple-element.1039) | copy-start | bytes 1540
  728.7 305.8 %copy-start.160 = (f32[128]{0:T(128)}, f32[128]{0:T(128)S(1)}, u32[]{:S(2)}) copy-start(f32[128]{0:T(128)S(1)} %get-tuple-element.1038) | copy-start | bytes 1540
  728.7 312.3 %copy-start.159 = (f32[128]{0:T(128)}, f32[128]{0:T(128)S(1)}, u32[]{:S(2)}) copy-start(f32[128]{0:T(128)S(1)} %get-tuple-element.1037) | copy-start | bytes 1540
  887.3 272.3 %reduce-scatter.12.cloned.1.call-start = ((), (), s32[]{:S(2)}) async-start(), calls=%async_computation.20 | async-start | bytes 3538944 | tf_op jit(solution)/shard_map/reduce_scatter | solution.py:314
  985.5 175.9 %reduce-scatter.18.cloned.1.call-start = ((), (), s32[]{:S(2)}) async-start(), calls=%async_computation.23 | async-start | bytes 3538944 | tf_op jit(solution)/shard_map/reduce_scatter | solution.py:317
  986.2 227.6 %reduce-scatter.14.cloned.1.call-start = ((), (), s32[]{:S(2)}) async-start(), calls=%async_computation.21 | async-start | bytes 3538944 | tf_op jit(solution)/shard_map/reduce_scatter | solution.py:317
  986.8 478.3 %reduce-scatter.30.cloned.1.call-start = ((), (), s32[]{:S(2)}) async-start(), calls=%async_computation.29 | async-start | bytes 25952256 | tf_op jit(solution)/shard_map/reduce_scatter | solution.py:350
  1047.8 855.9 %reduce-scatter.28.cloned.1.call-start = ((), (), s32[]{:S(2)}) async-start(), calls=%async_computation.28 | async-start | bytes 51904512 | tf_op jit(solution)/shard_map/reduce_scatter | solution.py:349
  1140.8 883.2 %reduce-scatter.26.cloned.1.call-start = ((), (), s32[]{:S(2)}) async-start(), calls=%async_computation.27 | async-start | bytes 6488064 | tf_op jit(solution)/shard_map/reduce_scatter | solution.py:348
  1146.7 1038.5 %reduce-scatter.24.cloned.1.call-start = ((), (), s32[]{:S(2)}) async-start(), calls=%async_computation.26 | async-start | bytes 12976128 | tf_op jit(solution)/shard_map/reduce_scatter | solution.py:347
  1156.1 1133.8 %reduce-scatter.22.cloned.1.call-start = ((), (), s32[]{:S(2)}) async-start(), calls=%async_computation.25 | async-start | bytes 2433024 | tf_op jit(solution)/shard_map/reduce_scatter | solution.py:344
  1159.5 1254.8 %reduce-scatter.20.cloned.1.call-start = ((), (), s32[]{:S(2)}) async-start(), calls=%async_computation.24 | async-start | bytes 7299072 | tf_op jit(solution)/shard_map/reduce_scatter | solution.py:343
  (165 other events, 1767.4 us)
Sparse Core Ops, SparseCore 0:
  11.0 63.0 all-gather.11
  87.6 45.1 all-gather.27
  134.9 42.5 all-gather.13
  179.5 42.3 all-gather.15
  224.7 53.1 all-gather.17
  280.6 43.0 all-gather.29
  326.7 68.4 all-gather.19
  398.2 57.5 all-gather.21
  459.2 153.5 all-gather.23
  615.4 94.3 all-gather.25
  887.4 73.0 reduce-scatter.15
  985.6 73.0 reduce-scatter.11
  1062.3 73.8 reduce-scatter.17
  1139.7 74.1 reduce-scatter.13
  1220.1 244.9 reduce-scatter.29
  1472.5 431.1 reduce-scatter.27
  1910.7 113.3 reduce-scatter.25
  2030.5 154.6 reduce-scatter.23
  2191.8 98.0 reduce-scatter.21
  2296.0 118.2 reduce-scatter.19
where the time goes:
time: 2430 us; the launch traced here: 2420 us
  waiting for transfers between devices  1580 us (65%)
  matrix products  491 us (20%)
  blocking collectives  149 us (6%)
  local copies, waits for them, and re-layouts  114 us (5%)
  other arithmetic  68.5 us (3%)
    reduce_scatter x1, waiting for transfers between devices, shards(): lax.psum_scatter(running[7], ('dp', 'ctx'), scatter_dimension=0, tiled=True)  436 us
    reduce_scatter x1, waiting for transfers between devices, shards(): lax.psum_scatter(running[8], ('dp', 'ctx'), scatter_dimension=0, tiled=True)  192 us
    reduce_scatter x1, waiting for transfers between devices, shards(): lax.psum_scatter(running[5], ('dp', 'ctx'), scatter_dimension=0, tiled=True)  161 us
    all_gather x1, waiting for transfers between devices, shards(): lax.all_gather(expert_in, ('dp', 'ctx'), axis=0, tiled=True)  143 us
    reduce_scatter x1, waiting for transfers between devices, shards(): lax.psum_scatter(running[1], ('dp', 'ctx'), scatter_dimension=0, tiled=True)  124 us
    reduce_scatter x1, waiting for transfers between devices, shards(): lax.psum_scatter(running[6], ('dp', 'ctx'), scatter_dimension=0, tiled=True)  117 us
    reduce_scatter x1, waiting for transfers between devices, shards(): lax.psum_scatter(running[2], ('dp', 'ctx'), scatter_dimension=0, tiled=True)  105 us
    dot_general x10, matrix products, swiglu_backward(): jnp.einsum('scd,scf->df', normed, pre_grad, preferred_element_type=jnp.fl...  83.5 us
  transfers between devices with their start and end apart: 20, of which 16 were waited for; matrix products, arithmetic and copies ran while one was open for 20% of the time, Pallas kernels for 0%

commit v1 on v0

v1 whole, which is shorter than its diff:
```python
import functools

import jax
import jax.numpy as jnp
import numpy as np
from jax import lax
from jax.experimental import pallas as pl
from jax.experimental.pallas import tpu as pltpu
from jax.sharding import PartitionSpec as P

HEADS = 12
HEAD_DIM = 64
FF = 2048
EPSILON = 1e-05
HALVES = 2
QUERY_ROWS = 256
MIX_ROWS = 16
MESH = pl.DeviceIdType.MESH
BF16 = jnp.bfloat16
F32 = jnp.float32


def round_up(value, step):
    return -(-value // step) * step


class Plan:
    def __init__(self, dp, ctx, block, width, experts):
        self.dp, self.ctx, self.block, self.width, self.experts = dp, ctx, block, width, experts
        self.quad = ctx // HALVES
        self.devices = dp * ctx
        self.group = dp * self.quad
        self.slots = ctx * block
        self.rows = width // self.devices
        self.heads = -(-HEADS // self.quad)
        self.head_cols = self.heads * HEAD_DIM
        self.qkv_cols = 3 * self.head_cols
        self.wide = round_up(self.qkv_cols + 2 + experts, 128)
        self.own_hidden = FF // self.devices
        self.branches = 1 + experts
        self.hidden = self.branches * HALVES * self.own_hidden
        self.hidden_pad = round_up(self.hidden, 128)
        self.local = HALVES * block


def place():
    return lax.axis_index("dp"), lax.axis_index("ctx")


def params(collective_id=None, limit=60 * 1024 * 1024):
    if collective_id is None:
        return pltpu.CompilerParams(vmem_limit_bytes=limit)
    return pltpu.CompilerParams(
        vmem_limit_bytes=limit, collective_id=collective_id, has_side_effects=True
    )


def remote(src, dst, send_sem, recv_sem, device):
    return pltpu.make_async_remote_copy(
        src_ref=src,
        dst_ref=dst,
        send_sem=send_sem,
        recv_sem=recv_sem,
        device_id=device,
        device_id_type=MESH,
    )


def meet(devices):
    barrier = pltpu.get_barrier_semaphore()
    for device in devices:
        pl.semaphore_signal(barrier, inc=1, device_id=device, device_id_type=MESH)
    pl.semaphore_wait(barrier, len(devices))


def other_devices(plan, dp, ctx):
    flat = dp * plan.ctx + ctx
    result = []
    for step in range(1, plan.devices):
        target = lax.rem(flat + step, plan.devices)
        result.append((lax.div(target, plan.ctx), lax.rem(target, plan.ctx)))
    return result


def quad_members(plan, half, member):
    return [
        (half * plan.quad + lax.rem(member + step, plan.quad), lax.rem(member + step, plan.quad))
        for step in range(1, plan.quad)
    ]


VMEM = pl.BlockSpec(memory_space=pltpu.VMEM)
HBM = pl.BlockSpec(memory_space=pl.ANY)
DMA = pltpu.SemaphoreType.DMA


def spread_kernel(plan, tok, wq, win, xs, wall, winh, x_send, x_recv, q_send, q_recv, f_send, f_recv):
    dp, ctx = place()
    half, member = lax.div(ctx, plan.quad), lax.rem(ctx, plan.quad)
    far = (1 - half) * plan.quad + member
    flat = dp * plan.ctx + ctx
    mine = dp * plan.quad + member
    others = other_devices(plan, dp, ctx)
    meet(others)
    copies = []

    swap = remote(tok.at[1 - half], xs.at[ctx], x_send.at[0], x_recv.at[0], (dp, far))
    swap.start()
    members = quad_members(plan, half, member)
    count = len(members)
    for i, (peer, _) in enumerate(members):
        copy = remote(tok.at[half], xs.at[ctx], x_send.at[1 + i], x_recv.at[1 + i], (dp, peer))
        copy.start()
        copies.append(copy)
    for i, (tdp, tctx) in enumerate(others):
        copy = remote(
            wq.at[lax.rem(tctx, plan.quad)], wall.at[flat], q_send.at[i], q_recv.at[i], (tdp, tctx)
        )
        copy.start()
        copies.append(copy)
    for i in range(plan.group - 1):
        target = lax.rem(mine + 1 + i, plan.group)
        tdp, tmember = lax.div(target, plan.quad), lax.rem(target, plan.quad)
        copy = remote(
            win.at[target],
            winh.at[mine],
            f_send.at[i],
            f_recv.at[i],
            (tdp, half * plan.quad + tmember),
        )
        copy.start()
        copies.append(copy)
    xs[pl.ds(ctx, 1)] = tok[pl.ds(half, 1)]
    wall[pl.ds(flat, 1)] = wq[pl.ds(member, 1)]
    winh[pl.ds(mine, 1)] = win[pl.ds(mine, 1)]
    swap.wait()
    for i, (peer, _) in enumerate(members):
        copy = remote(
            xs.at[far], xs.at[far], x_send.at[1 + count + i], x_recv.at[1 + count + i], (dp, peer)
        )
        copy.start()
        copies.append(copy)
    for copy in copies:
        copy.wait()


def spread(plan, tok, wq, win):
    count = 2 * plan.quad - 1
    return pl.pallas_call(
        functools.partial(spread_kernel, plan),
        out_shape=(
            jax.ShapeDtypeStruct((plan.ctx, plan.block, plan.width), BF16),
            jax.ShapeDtypeStruct((plan.devices, plan.rows, plan.wide), BF16),
            jax.ShapeDtypeStruct((plan.group, plan.rows, 2 * plan.hidden_pad), BF16),
        ),
        in_specs=[VMEM] * 3,
        out_specs=(VMEM,) * 3,
        scratch_shapes=[
            DMA((count,)),
            DMA((count,)),
            DMA((plan.devices - 1,)),
            DMA((plan.devices - 1,)),
            DMA((plan.group - 1,)),
            DMA((plan.group - 1,)),
        ],
        compiler_params=params(1),
        name="spread",
    )(tok, wq, win)


def to_slots_kernel(plan, src, dst, send, recv):
    dp, ctx = place()
    half, member = lax.div(ctx, plan.quad), lax.rem(ctx, plan.quad)
    far = (1 - half) * plan.quad + member
    members = quad_members(plan, half, member)
    meet([(dp, peer) for peer, _ in members])
    copies = []
    for i, (peer, to) in enumerate(members):
        for j, at in enumerate((ctx, far)):
            copy = remote(
                src.at[to, j], dst.at[at], send.at[2 * i + j], recv.at[2 * i + j], (dp, peer)
            )
            copy.start()
            copies.append(copy)
    dst[pl.ds(ctx, 1)] = src[pl.ds(member, 1), 0]
    dst[pl.ds(far, 1)] = src[pl.ds(member, 1), 1]
    for copy in copies:
        copy.wait()


def to_slots(plan, value, collective_id):
    count = 2 * (plan.quad - 1)
    return pl.pallas_call(
        functools.partial(to_slots_kernel, plan),
        out_shape=jax.ShapeDtypeStruct((plan.ctx, plan.block, value.shape[-1]), value.dtype),
        in_specs=[VMEM],
        out_specs=VMEM,
        scratch_shapes=[DMA((count,)), DMA((count,))],
        compiler_params=params(collective_id),
        name="to_slots",
    )(value)


def send_to_owners(plan, dp, half, member, src, dst, send, recv):
    copies = []
    for i, (peer, to) in enumerate(quad_members(plan, half, member)):
        for j, at in enumerate((half * plan.quad + to, (1 - half) * plan.quad + to)):
            copy = remote(
                src.at[at], dst.at[member, j], send.at[2 * i + j], recv.at[2 * i + j], (dp, peer)
            )
            copy.start()
            copies.append(copy)
    return copies


def to_owners_kernel(plan, src, dst, send, recv):
    dp, ctx = place()
    half, member = lax.div(ctx, plan.quad), lax.rem(ctx, plan.quad)
    far = (1 - half) * plan.quad + member
    meet([(dp, peer) for peer, _ in quad_members(plan, half, member)])
    copies = send_to_owners(plan, dp, half, member, src, dst, send, recv)
    dst[pl.ds(member, 1), 0] = src[pl.ds(ctx, 1)]
    dst[pl.ds(member, 1), 1] = src[pl.ds(far, 1)]
    for copy in copies:
        copy.wait()


def to_owners(plan, value, collective_id):
    count = 2 * (plan.quad - 1)
    return pl.pallas_call(
        functools.partial(to_owners_kernel, plan),
        out_shape=jax.ShapeDtypeStruct((plan.quad, 2, plan.block, value.shape[-1]), value.dtype),
        in_specs=[VMEM],
        out_specs=VMEM,
        scratch_shapes=[DMA((count,)), DMA((count,))],
        compiler_params=params(collective_id),
        name="to_owners",
    )(value)


def collect_kernel(plan, dnp, dwq, dwo, dwin, rdn, rwq, rwo, rwin, n_send, n_recv, q_send, q_recv, o_send, o_recv, f_send, f_recv):
    dp, ctx = place()
    half, member = lax.div(ctx, plan.quad), lax.rem(ctx, plan.quad)
    far = (1 - half) * plan.quad + member
    flat = dp * plan.ctx + ctx
    mine = dp * plan.quad + member
    others = other_devices(plan, dp, ctx)
    meet(others)
    copies = send_to_owners(plan, dp, half, member, dnp, rdn, n_send, n_recv)
    for i, (tdp, tctx) in enumerate(others):
        to = tdp * plan.ctx + tctx
        copy = remote(dwq.at[to], rwq.at[flat], q_send.at[i], q_recv.at[i], (tdp, tctx))
        copy.start()
        copies.append(copy)
        copy = remote(dwo.at[to], rwo.at[flat], o_send.at[i], o_recv.at[i], (tdp, tctx))
        copy.start()
        copies.append(copy)
    for i in range(plan.group - 1):
        target = lax.rem(mine + 1 + i, plan.group)
        tdp, tmember = lax.div(target, plan.quad), lax.rem(target, plan.quad)
        copy = remote(
            dwin.at[target],
            rwin.at[mine],
            f_send.at[i],
            f_recv.at[i],
            (tdp, half * plan.quad + tmember),
        )
        copy.start()
        copies.append(copy)
    rdn[pl.ds(member, 1), 0] = dnp[pl.ds(ctx, 1)]
    rdn[pl.ds(member, 1), 1] = dnp[pl.ds(far, 1)]
    rwq[pl.ds(flat, 1)] = dwq[pl.ds(flat, 1)]
    rwo[pl.ds(flat, 1)] = dwo[pl.ds(flat, 1)]
    rwin[pl.ds(mine, 1)] = dwin[pl.ds(mine, 1)]
    for copy in copies:
        copy.wait()


def collect(plan, dnp, dwq, dwo, dwin):
    count = 2 * (plan.quad - 1)
    return pl.pallas_call(
        functools.partial(collect_kernel, plan),
        out_shape=(
            jax.ShapeDtypeStruct((plan.quad, 2, plan.block, plan.width), BF16),
            jax.ShapeDtypeStruct(dwq.shape, BF16),
            jax.ShapeDtypeStruct(dwo.shape, BF16),
            jax.ShapeDtypeStruct(dwin.shape, BF16),
        ),
        in_specs=[VMEM] * 4,
        out_specs=(VMEM,) * 4,
        scratch_shapes=[
            DMA((count,)),
            DMA((count,)),
            DMA((plan.devices - 1,)),
            DMA((plan.devices - 1,)),
            DMA((plan.devices - 1,)),
            DMA((plan.devices - 1,)),
            DMA((plan.group - 1,)),
            DMA((plan.group - 1,)),
        ],
        compiler_params=params(6),
        name="collect",
    )(dnp, dwq, dwo, dwin)


class Grid:
    def __init__(self, plan):
        self.plan = plan
        self.sizes = {"y": plan.dp // 2, "high": plan.quad // 2, "low": 2}

    def here(self):
        dp, ctx = place()
        member = lax.rem(ctx, self.plan.quad)
        return {
            "core": lax.rem(dp, 2),
            "y": lax.div(dp, 2),
            "high": lax.div(member, 2),
            "low": lax.rem(member, 2),
            "half": lax.div(ctx, self.plan.quad),
        }

    def device(self, at):
        return (
            at["y"] * 2 + at["core"],
            at["half"] * self.plan.quad + at["high"] * 2 + at["low"],
        )

    def block(self, at):
        return (at["y"] * 2 + at["core"]) * self.plan.quad + at["high"] * 2 + at["low"]

    def moved(self, at, axis, step):
        result = dict(at)
        if axis == "core":
            result["core"] = 1 - at["core"]
        else:
            result[axis] = lax.rem(at[axis] + step, self.sizes[axis])
        return result

    def peers(self, at):
        result = [self.moved(at, "core", 1)]
        for axis, size in self.sizes.items():
            result += [self.moved(at, axis, step) for step in range(1, size)]
        return [self.device(peer) for peer in result]

    def slot(self, offsets):
        return (offsets["y"] * self.sizes["high"] + offsets["high"]) * 2 + offsets["low"]


GATHER_ORDERS = (("high", "low", "y"), ("low", "y", "high"))


def gather_kernel(plan, src, dst, send, recv, core_send, core_recv):
    grid = Grid(plan)
    at = grid.here()
    meet(grid.peers(at))
    dst[pl.ds(grid.block(at), 1)] = src[...][None]
    zero = {"y": 0, "high": 0, "low": 0}

    def run(order):
        levels = [[dict(zero)], [], [], []]
        for level, axis in enumerate(order):
            base = [o for group in levels[: level + 1] for o in group]
            for offsets in base:
                for step in range(1, grid.sizes[axis]):
                    levels[level + 1].append({**offsets, axis: step})
        sends = []
        counter = [0]

        def absolute(offsets):
            where = dict(at)
            for axis, step in offsets.items():
                if step:
                    where = grid.moved(where, axis, step)
            return where

        for level, group in enumerate(levels):
            for offsets in group:
                where = absolute(offsets)
                block = grid.block(where)
                if level:
                    remote(dst.at[block], dst.at[block], send.at[0], recv.at[grid.slot(offsets)], grid.device(at)).wait_recv()
                source = src if level == 0 else dst.at[block]
                for axis in order[level:]:
                    for step in range(1, grid.sizes[axis]):
                        seen = {**offsets, axis: grid.sizes[axis] - step}
                        copy = remote(
                            source,
                            dst.at[block],
                            send.at[counter[0]],
                            recv.at[grid.slot(seen)],
                            grid.device(grid.moved(at, axis, step)),
                        )
                        copy.start()
                        counter[0] += 1
                        sends.append(copy)
                copy = remote(
                    source,
                    dst.at[block],
                    core_send.at[grid.slot(offsets)],
                    core_recv.at[grid.slot(offsets)],
                    grid.device(grid.moved(at, "core", 1)),
                )
                copy.start()
                sends.append(copy)
        for copy in sends:
            copy.wait_send()
        for slot in range(plan.group // 2):
            remote(src, dst.at[0], core_send.at[slot], core_recv.at[slot], grid.device(at)).wait_recv()

    for color, order in enumerate(GATHER_ORDERS):
        pl.when(at["core"] == color)(functools.partial(run, order))


def gather_sends(plan, order):
    sizes = Grid(plan).sizes
    held, total = 1, 0
    for axis in order:
        total += held * (sizes[axis] - 1)
        held *= sizes[axis]
    return total


def gather(plan, block, collective_id):
    half = plan.group // 2
    count = max(gather_sends(plan, order) for order in GATHER_ORDERS)
    return pl.pallas_call(
        functools.partial(gather_kernel, plan),
        out_shape=jax.ShapeDtypeStruct((plan.group,) + block.shape, block.dtype),
        in_specs=[VMEM],
        out_specs=VMEM,
        scratch_shapes=[DMA((count,)), DMA((half,)), DMA((half,)), DMA((half,))],
        compiler_params=params(collective_id),
        name="gather",
    )(block)


def reduce_kernel(plan, src, out, work, core_buf, bufs, load_sem, core_send, core_recv, send, recv):
    grid = Grid(plan)
    at = grid.here()
    zero = {"y": 0, "high": 0, "low": 0}
    meet(grid.peers(at))

    def run(order):
        levels = [[], [], [], []]
        held = [dict(zero)]
        levels[3] = [dict(zero)]
        for level in (2, 1, 0):
            axis = order[level]
            base = [o for later in levels[level + 1 :] for o in later]
            levels[level] = [
                {**offsets, axis: step} for offsets in base for step in range(1, grid.sizes[axis])
            ]
        del held

        def absolute(offsets):
            where = dict(at)
            for axis, step in offsets.items():
                if step:
                    where = grid.moved(where, axis, step)
            return where

        sequence = [o for group in levels for o in group]
        partner = grid.device(grid.moved(at, "core", 1))
        core_copies = []
        loads = []
        for offsets in sequence:
            where = absolute(offsets)
            slot = grid.slot(offsets)
            copy = remote(
                src.at[grid.block(grid.moved(where, "core", 1))],
                core_buf.at[slot],
                core_send.at[slot],
                core_recv.at[slot],
                partner,
            )
            copy.start()
            core_copies.append(copy)
            load = pltpu.make_async_copy(
                src.at[grid.block(where)], work.at[slot], load_sem.at[slot]
            )
            load.start()
            loads.append(load)
        arrived = {}
        sends = []
        index = 0
        position = 0
        for level in range(4):
            for offsets in levels[level]:
                slot = grid.slot(offsets)
                core_copies[position].wait_recv()
                loads[position].wait()
                position += 1
                total = work[slot].astype(F32) + core_buf[slot].astype(F32)
                for buffer in arrived.get(slot, ()):
                    remote(work.at[slot], bufs.at[buffer], send.at[0], recv.at[buffer], partner).wait_recv()
                    total = total + bufs[buffer].astype(F32)
                if level == 3:
                    out[...] = total.astype(out.dtype)
                    continue
                work[slot] = total.astype(BF16)
                axis = order[level]
                step = offsets[axis]
                copy = remote(
                    work.at[slot],
                    bufs.at[index],
                    send.at[index],
                    recv.at[index],
                    grid.device(grid.moved(at, axis, step)),
                )
                copy.start()
                sends.append(copy)
                landing = grid.slot({**offsets, axis: 0})
                arrived.setdefault(landing, []).append(index)
                index += 1
        for copy in sends:
            copy.wait_send()
        for copy in core_copies:
            copy.wait_send()

    for color, order in enumerate(GATHER_ORDERS):
        pl.when(at["core"] == color)(functools.partial(run, order[::-1]))


def reduce(plan, blocks, collective_id):
    half = plan.group // 2
    shape = blocks.shape[1:]
    count = max(gather_sends(plan, order) for order in GATHER_ORDERS)
    return pl.pallas_call(
        functools.partial(reduce_kernel, plan),
        out_shape=jax.ShapeDtypeStruct(shape, F32),
        in_specs=[HBM],
        out_specs=VMEM,
        scratch_shapes=[
            pltpu.VMEM((half,) + shape, BF16),
            pltpu.VMEM((half,) + shape, BF16),
            pltpu.VMEM((count,) + shape, BF16),
            DMA((half,)),
            DMA((half,)),
            DMA((half,)),
            DMA((count,)),
            DMA((count,)),
        ],
        compiler_params=params(collective_id),
        name="reduce",
    )(blocks)


def nt(left, right):
    return lax.dot_general(left, right, (((1,), (1,)), ((), ())), preferred_element_type=F32)


def nn(left, right):
    return lax.dot_general(left, right, (((1,), (0,)), ((), ())), preferred_element_type=F32)


def tn(left, right):
    return lax.dot_general(left, right, (((0,), (0,)), ((), ())), preferred_element_type=F32)


def swapped_halves(value):
    lane = lax.broadcasted_iota(jnp.int32, value.shape, 1)
    first = lax.rem(lane, HEAD_DIM) < HEAD_DIM // 2
    half = HEAD_DIM // 2
    return jnp.where(
        first, pltpu.roll(value, 2 * HEAD_DIM - half, 1), pltpu.roll(value, half, 1)
    )


def masked_scores(q, k, first_row, length):
    scores = nt(q, k)
    row = lax.broadcasted_iota(jnp.int32, scores.shape, 0) + first_row
    col = lax.broadcasted_iota(jnp.int32, scores.shape, 1)
    return jnp.where((col <= row) & (col < length), scores, -1000000000.0)


def attend_kernel(plan, length_ref, x, gain, w, cosine, sine, mixed, normed, qk_out, v_out, lse_out, qkv):
    length = length_ref[0]
    rows = QUERY_ROWS
    slots = plan.slots
    for start in range(0, slots, rows):
        at = slice(start, start + rows)
        values = x[at].astype(F32)
        inverse = lax.rsqrt(jnp.mean(values * values, axis=-1, keepdims=True) + EPSILON)
        normed[at] = (values * inverse * gain[...]).astype(BF16)
        qkv[at] = nn(normed[at], w[...])
    heads = plan.heads
    qk_width = 2 * HEAD_DIM
    for head in range(heads):
        cols = slice(head * qk_width, (head + 1) * qk_width)
        qk = qkv[:, cols]
        qk_out[:, cols] = (qk * cosine[...] + swapped_halves(qk) * sine[...]).astype(BF16)
    v_cols = slice(heads * qk_width, heads * 3 * HEAD_DIM)
    v_out[...] = qkv[:, v_cols].astype(BF16)
    for head in range(heads):
        base = head * qk_width
        for start in range(0, slots, rows):
            at = slice(start, start + rows)
            end = start + rows
            q = qk_out[at, base : base + HEAD_DIM] * BF16(0.125)
            k = qk_out[:end, base + HEAD_DIM : base + qk_width]
            v = v_out[:end, head * HEAD_DIM : (head + 1) * HEAD_DIM]
            scores = masked_scores(q, k, start, length)
            top = jnp.max(scores, axis=-1, keepdims=True)
            raised = jnp.exp(scores - top)
            total = jnp.sum(raised, axis=-1, keepdims=True)
            lse_out[head, at] = top + jnp.log(total)
            probs = (raised * (1.0 / total)).astype(BF16)
            mixed[at, head * HEAD_DIM : (head + 1) * HEAD_DIM] = nn(probs, v).astype(BF16)


def attend(plan, length, x, gain, w, cosine, sine):
    slots, heads = plan.slots, plan.heads
    return pl.pallas_call(
        functools.partial(attend_kernel, plan),
        out_shape=(
            jax.ShapeDtypeStruct((slots, plan.head_cols), BF16),
            jax.ShapeDtypeStruct((slots, plan.width), BF16),
            jax.ShapeDtypeStruct((slots, 2 * plan.head_cols), BF16),
            jax.ShapeDtypeStruct((slots, plan.head_cols), BF16),
            jax.ShapeDtypeStruct((heads, slots, 1), F32),
        ),
        in_specs=[pl.BlockSpec(memory_space=pltpu.SMEM)] + [VMEM] * 5,
        out_specs=(VMEM,) * 5,
        scratch_shapes=[pltpu.VMEM((slots, plan.wide), F32)],
        compiler_params=params(),
        name="attend",
    )(length, x, gain, w, cosine, sine)


def attend_back_kernel(plan, length_ref, x, w, cosine, sine, normed, qk_in, v_in, lse, dmixed, dnp, dw, gain_grad, dqkv, dq_acc, dk_acc, dv_acc):
    length = length_ref[0]
    rows, slots, heads = QUERY_ROWS, plan.slots, plan.heads
    qk_width = 2 * HEAD_DIM
    dqkv[...] = jnp.zeros_like(dqkv)
    for head in range(heads):
        base = head * qk_width
        v_cols = slice(head * HEAD_DIM, (head + 1) * HEAD_DIM)
        for start in range(slots - rows, -1, -rows):
            at = slice(start, start + rows)
            end = start + rows
            q = qk_in[at, base : base + HEAD_DIM] * BF16(0.125)
            k = qk_in[:end, base + HEAD_DIM : base + qk_width]
            v = v_in[:end, v_cols]
            upstream = dmixed[at, v_cols]
            probs = jnp.exp(masked_scores(q, k, start, length) - lse[head, at])
            dv = tn(probs.astype(BF16), upstream)
            prob_grad = nt(upstream, v)
            inner = jnp.sum(probs * prob_grad, axis=-1, keepdims=True)
            score_grad = (probs * (prob_grad - inner)).astype(BF16)
            dq_acc[at] = nn(score_grad, k) * 0.125
            dk = tn(score_grad, q)
            if end == slots:
                dk_acc[...] = dk
                dv_acc[...] = dv
            else:
                dk_acc[:end] += dk
                dv_acc[:end] += dv
        dqk = jnp.concatenate([dq_acc[...], dk_acc[...]], axis=-1)
        dqkv[:, base : base + qk_width] = (
            dqk * cosine[...] - swapped_halves(dqk) * sine[...]
        ).astype(BF16)
        v_base = heads * qk_width + head * HEAD_DIM
        dqkv[:, v_base : v_base + HEAD_DIM] = dv_acc[...].astype(BF16)
    dw[...] = tn(normed[...], dqkv[...]).astype(dw.dtype)
    gains = jnp.zeros((1, plan.width), F32)
    for start in range(0, slots, rows):
        at = slice(start, start + rows)
        part = nt(dqkv[at], w[...])
        dnp[at] = part.astype(BF16)
        values = x[at].astype(F32)
        inverse = lax.rsqrt(jnp.mean(values * values, axis=-1, keepdims=True) + EPSILON)
        gains = gains + jnp.sum(part * values * inverse, axis=0, keepdims=True)
    gain_grad[...] = gains


def attend_back(plan, length, x, w, cosine, sine, normed, qk, v, lse, dmixed):
    slots = plan.slots
    return pl.pallas_call(
        functools.partial(attend_back_kernel, plan),
        out_shape=(
            jax.ShapeDtypeStruct((slots, plan.width), BF16),
            jax.ShapeDtypeStruct((plan.width, plan.wide), F32),
            jax.ShapeDtypeStruct((1, plan.width), F32),
        ),
        in_specs=[pl.BlockSpec(memory_space=pltpu.SMEM)] + [VMEM] * 9,
        out_specs=(VMEM,) * 3,
        scratch_shapes=[
            pltpu.VMEM((slots, plan.wide), BF16),
            pltpu.VMEM((slots, HEAD_DIM), F32),
            pltpu.VMEM((slots, HEAD_DIM), F32),
            pltpu.VMEM((slots, HEAD_DIM), F32),
        ],
        compiler_params=params(),
        name="attend_back",
    )(length, x, w, cosine, sine, normed, qk, v, lse, dmixed)


def ffn_kernel(plan, members, n2x, gy, w_in, w_out, pick, out, n2g, dw_in, dw_out):
    hidden, local = plan.hidden_pad, plan.local

    @pl.when(pl.program_id(0) == 0)
    def start():
        dw_in[...] = jnp.zeros_like(dw_in)
        dw_out[...] = jnp.zeros_like(dw_out)

    tokens = members * local
    width = plan.width
    normed = n2x[:, :local].reshape(tokens, width)
    upstream = gy[...].reshape(tokens, width)
    mixing = jnp.concatenate(
        [tn(n2x[i, local:, :local], pick[...]) for i in range(members)], axis=0
    )
    pre = nn(normed, w_in[...])
    gate, up = pre[:, :hidden], pre[:, hidden:]
    sigmoid = jax.nn.sigmoid(gate)
    silu = gate * sigmoid
    act = (silu * up).astype(BF16).astype(F32)
    act_mixed = (act * mixing).astype(BF16)
    out[...] = nn(act_mixed, w_out[...]).astype(BF16).reshape(members, local, width)
    act_grad = nt(upstream, w_out[...])
    choice = nt(pick[...], (act * act_grad).astype(BF16)).astype(BF16)
    act_grad = act_grad * mixing
    gate_grad = act_grad * up * sigmoid * (1.0 + gate * (1.0 - sigmoid))
    pre_grad = jnp.concatenate([gate_grad, act_grad * silu], axis=-1).astype(BF16)
    n2g[:, :local] = nt(pre_grad, w_in[...]).astype(BF16).reshape(members, local, width)
    pad = jnp.zeros((MIX_ROWS, width - local), BF16)
    for i in range(members):
        n2g[i, local:] = jnp.concatenate(
            [choice[:, i * local : (i + 1) * local], pad], axis=-1
        )
    dw_in[...] += tn(normed, pre_grad)
    dw_out[...] += tn(act_mixed, upstream)


def ffn(plan, n2x, gy, w_in, w_out, pick):
    members = 2
    local, width, hidden = plan.local, plan.width, plan.hidden_pad
    whole = lambda i: (0, 0)
    part = lambda i: (i, 0, 0)
    return pl.pallas_call(
        functools.partial(ffn_kernel, plan, members),
        grid=(plan.group // members,),
        out_shape=(
            jax.ShapeDtypeStruct((plan.group, local, width), BF16),
            jax.ShapeDtypeStruct((plan.group, local + MIX_ROWS, width), BF16),
            jax.ShapeDtypeStruct((width, 2 * hidden), F32),
            jax.ShapeDtypeStruct((hidden, width), F32),
        ),
        in_specs=[
            pl.BlockSpec((members, local + MIX_ROWS, width), part),
            pl.BlockSpec((members, local, width), part),
            pl.BlockSpec((width, 2 * hidden), whole),
            pl.BlockSpec((hidden, width), whole),
            pl.BlockSpec((MIX_ROWS, hidden), whole),
        ],
        out_specs=(
            pl.BlockSpec((members, local, width), part),
            pl.BlockSpec((members, local + MIX_ROWS, width), part),
            pl.BlockSpec((width, 2 * hidden), whole),
            pl.BlockSpec((hidden, width), whole),
        ),
        compiler_params=params(),
        name="ffn",
    )(n2x, gy, w_in, w_out, pick)


def by_half(half, mine, far, axis):
    return jnp.where(
        half == 0, jnp.stack([mine, far], axis), jnp.stack([far, mine], axis)
    )


def rope_tables(plan):
    half = HEAD_DIM // 2
    frequency = np.float32(10000.0) ** (-np.arange(half, dtype=np.float32) / np.float32(half))
    angles = np.arange(plan.slots, dtype=np.float32)[:, None] * frequency[None, :]
    cosine = np.cos(angles.astype(np.float64)).astype(np.float32)
    sine = np.sin(angles.astype(np.float64)).astype(np.float32)
    return np.tile(cosine, (1, 4)), np.tile(np.concatenate([-sine, sine], 1), (1, 2))


def pick_table(plan):
    table = np.zeros((MIX_ROWS, plan.hidden_pad), np.float32)
    span = HALVES * plan.own_hidden
    for expert in range(plan.experts):
        cols = slice((1 + expert) * span, (2 + expert) * span)
        table[expert, cols] = 1.0
        table[plan.experts + expert, cols] = 1.0
    table[2 * plan.experts, :span] = 1.0
    return jnp.asarray(table, BF16)


def pack_qkv(plan, attn_in, attn_gain, ffn_gain, router):
    rows, quad, heads = plan.rows, plan.quad, plan.heads
    qkv = attn_in.reshape(rows, 3, HEADS, HEAD_DIM)
    qkv = jnp.pad(qkv, ((0, 0), (0, 0), (0, quad * heads - HEADS), (0, 0)))
    qkv = qkv.reshape(rows, 3, quad, heads, HEAD_DIM)
    qk = jnp.transpose(qkv[:, :2], (2, 0, 3, 1, 4)).reshape(quad, rows, 2 * plan.head_cols)
    v = jnp.transpose(qkv[:, 2], (1, 0, 2, 3)).reshape(quad, rows, plan.head_cols)
    extra = jnp.concatenate([attn_gain[:, None], ffn_gain[:, None], router], axis=1)
    extra = jnp.pad(extra, ((0, 0), (0, plan.wide - plan.qkv_cols - extra.shape[1])))
    extra = jnp.broadcast_to(extra[None], (quad,) + extra.shape)
    return jnp.concatenate([qk, v, extra], axis=-1)


def unpack_qkv(plan, packed):
    rows, quad, heads = plan.rows, plan.quad, plan.heads
    qk = packed[..., : 2 * plan.head_cols].reshape(quad, rows, heads, 2, HEAD_DIM)
    v = packed[..., 2 * plan.head_cols : plan.qkv_cols].reshape(quad, rows, heads, 1, HEAD_DIM)
    qkv = jnp.transpose(jnp.concatenate([qk, v], axis=3), (1, 3, 0, 2, 4))
    qkv = qkv.reshape(rows, 3, quad * heads, HEAD_DIM)[:, :, :HEADS]
    return qkv.reshape(rows, 3 * HEADS * HEAD_DIM)


def pack_in(plan, dense_in, expert_in):
    rows, own = plan.rows, plan.own_hidden
    both = jnp.concatenate([dense_in[:, None], expert_in], axis=1)
    both = both.reshape(rows, plan.branches, 2, plan.dp, HALVES, plan.quad, own)
    both = jnp.transpose(both, (3, 5, 0, 2, 1, 4, 6))
    both = both.reshape(plan.group, rows, 2, plan.hidden)
    both = jnp.pad(both, ((0, 0), (0, 0), (0, 0), (0, plan.hidden_pad - plan.hidden)))
    return both.reshape(plan.group, rows, 2 * plan.hidden_pad)


def unpack_in(plan, packed):
    rows, own = plan.rows, plan.own_hidden
    both = packed.reshape(plan.group, rows, 2, plan.hidden_pad)[..., : plan.hidden]
    both = both.reshape(plan.dp, plan.quad, rows, 2, plan.branches, HALVES, own)
    both = jnp.transpose(both, (2, 4, 3, 0, 5, 1, 6))
    both = both.reshape(rows, plan.branches, 2 * FF).astype(F32)
    return both[:, 0], both[:, 1:]


def shards(
    tokens,
    lengths,
    routes,
    cotangent,
    attn_gain,
    attn_in,
    attn_out,
    ffn_gain,
    router,
    dense_in,
    dense_out,
    expert_in,
    expert_out,
):
    micro, seqs, block, width = tokens.shape
    experts = expert_in.shape[1]
    plan = Plan(lax.axis_size("dp"), lax.axis_size("ctx"), block, width, experts)
    assert micro == HALVES and seqs == 1 and plan.ctx % 4 == 0 and plan.dp % 2 == 0
    quad, local = plan.quad, plan.local
    dp, ctx = place()
    half, member = lax.div(ctx, quad), lax.rem(ctx, quad)
    across = [(i, (i + quad) % plan.ctx) for i in range(plan.ctx)]

    def swap(value):
        return lax.ppermute(value, "ctx", across)

    def pick_mine(value):
        return lax.dynamic_index_in_dim(value, half, 0, keepdims=False)

    def pick_far(value):
        return lax.dynamic_index_in_dim(value, 1 - half, 0, keepdims=False)

    cot, route = cotangent[:, 0], routes[:, 0]
    length = pick_mine(lengths)
    out_own = jnp.concatenate([dense_out[:, None], expert_out], axis=1)
    out_own = jnp.transpose(out_own, (1, 0, 2))
    cot_local = jnp.stack([pick_mine(cot), swap(pick_far(cot))])
    route_local = jnp.stack([pick_mine(route), swap(pick_far(route))]).reshape(local, 2)
    out_far = swap(out_own)
    w_mix = lax.all_gather(attn_out, ("dp", "ctx"), axis=0, tiled=True)

    xs, wall, win_mine = spread(
        plan,
        tokens[:, 0],
        pack_qkv(plan, attn_in, attn_gain, ffn_gain, router),
        pack_in(plan, dense_in, expert_in),
    )
    win_far = swap(win_mine)

    x_seq = xs.reshape(plan.slots, width)
    w_seq = wall.reshape(width, plan.wide)
    extra = w_seq[:, plan.qkv_cols :]
    gain_one = extra[:, 0].astype(F32)[None]
    gain_two = extra[:, 1].astype(F32)[None]
    w_route = extra[:, 2 : 2 + experts]
    cosine, sine = (jnp.asarray(table) for table in rope_tables(plan))
    mixed_seq, normed_seq, qk, v, lse = attend(plan, length, x_seq, gain_one, w_seq, cosine, sine)
    mixed = to_owners(plan, mixed_seq.reshape(plan.ctx, block, plan.head_cols), 2)
    mixed = jnp.transpose(mixed, (1, 2, 0, 3)).reshape(local, quad * plan.head_cols)[:, :width]

    x = jnp.stack(
        [
            lax.dynamic_index_in_dim(xs, ctx, 0, keepdims=False),
            lax.dynamic_index_in_dim(xs, (1 - half) * quad + member, 0, keepdims=False),
        ]
    )
    x = x.reshape(local, width).astype(F32)
    middle = x + nn(mixed, w_mix)
    inverse_two = lax.rsqrt(jnp.mean(middle * middle, axis=-1, keepdims=True) + EPSILON)
    normed_two = (middle * inverse_two * gain_two).astype(BF16)
    logits = nn(normed_two, w_route)
    choose = (route_local[..., None] == jnp.arange(experts, dtype=jnp.int32)).astype(F32)
    picked = jnp.sum(choose * logits[:, None, :], axis=-1)
    gates = jax.nn.softmax(picked, axis=-1)
    mixing = jnp.sum(gates[..., None] * choose, axis=1)
    mixing_t = mixing.T
    mixing_high = mixing_t.astype(BF16)
    mixing_low = (mixing_t - mixing_high.astype(F32)).astype(BF16)
    mix_rows = jnp.concatenate(
        [
            mixing_high,
            mixing_low,
            jnp.ones((1, local), BF16),
            jnp.zeros((MIX_ROWS - 2 * experts - 1, local), BF16),
        ]
    )
    mix_rows = jnp.pad(mix_rows, ((0, 0), (0, width - local)))
    n2x = gather(plan, jnp.concatenate([normed_two, mix_rows]), 3)

    starts = jnp.stack([ctx, (1 - half) * quad + member]) * block
    slot = (starts[:, None] + jnp.arange(block, dtype=jnp.int32)[None]).reshape(local)
    valid = (slot < length[0]).astype(BF16)[:, None]
    grad_y = cot_local.reshape(local, width) * valid
    gy = gather(plan, grad_y, 4)

    rows_in = (plan.dp, quad, plan.rows, 2 * plan.hidden_pad)
    w_in = by_half(half, win_mine.reshape(rows_in), win_far.reshape(rows_in), 1)
    w_in = w_in.reshape(width, 2 * plan.hidden_pad)
    w_out = by_half(half, out_own, out_far, 1).reshape(plan.hidden, width)
    w_out = jnp.pad(w_out, ((0, plan.hidden_pad - plan.hidden), (0, 0)))
    out_part, n2g_part, dw_in, dw_out = ffn(plan, n2x, gy, w_in, w_out, pick_table(plan))
    n2g_sum = reduce(plan, n2g_part, 5)
    out_sum = reduce(plan, out_part, 7)
    activations = (middle + out_sum).astype(BF16).reshape(2, block, width)

    dw_out = dw_out[: plan.hidden].reshape(plan.branches, HALVES, plan.own_hidden, width)
    dw_out = jnp.moveaxis(dw_out, 1, 0)
    dw_out = pick_mine(dw_out) + swap(pick_far(dw_out).astype(BF16)).astype(F32)
    dw_in = dw_in.reshape(plan.dp, HALVES, quad, plan.rows, 2 * plan.hidden_pad)
    dw_in = jnp.moveaxis(dw_in, 1, 0)
    dw_in = pick_mine(dw_in) + swap(pick_far(dw_in).astype(BF16)).astype(F32)
    dw_in = dw_in.astype(BF16).reshape(plan.group, plan.rows, 2 * plan.hidden_pad)

    normed_two_grad = n2g_sum[:local]
    mixing_grad = n2g_sum[local : local + experts, :local].T
    choice_grad = jnp.sum(choose * mixing_grad[:, None, :], axis=-1)
    pick_grad = gates * (choice_grad - jnp.sum(gates * choice_grad, axis=-1, keepdims=True))
    logit_grad = jnp.sum(pick_grad[..., None] * choose, axis=1).astype(BF16)
    router_grad = tn(normed_two, logit_grad)
    normed_two_grad = normed_two_grad + nt(logit_grad, w_route)
    gain_two_grad = jnp.sum(normed_two_grad * middle * inverse_two, axis=0)
    scaled = normed_two_grad * gain_two
    middle_grad = (
        grad_y.astype(F32)
        + inverse_two * scaled
        - middle * inverse_two**3 * jnp.mean(scaled * middle, axis=-1, keepdims=True)
    )
    attn_grad = middle_grad.astype(BF16)
    dw_mix = tn(mixed, attn_grad).astype(BF16).reshape(plan.devices, plan.rows, width)
    mixed_grad = nt(attn_grad, w_mix).astype(BF16)
    mixed_grad = jnp.pad(mixed_grad, ((0, 0), (0, quad * plan.head_cols - width)))
    mixed_grad = mixed_grad.reshape(2, block, quad, plan.head_cols)
    dmixed = to_slots(plan, jnp.transpose(mixed_grad, (2, 0, 1, 3)), 8)
    dnp, dw_qkv, gain_one_grad = attend_back(
        plan,
        length,
        x_seq,
        w_seq,
        cosine,
        sine,
        normed_seq,
        qk,
        v,
        lse,
        dmixed.reshape(plan.slots, plan.head_cols),
    )
    small = jnp.concatenate([gain_one_grad.T, gain_two_grad[:, None], router_grad], axis=1)
    small = jnp.pad(small, ((0, 0), (0, plan.wide - plan.qkv_cols - small.shape[1])))
    dw_qkv = jnp.concatenate([dw_qkv[:, : plan.qkv_cols], small], axis=1).astype(BF16)
    dn, r_qkv, r_mix, r_in = collect(
        plan,
        dnp.reshape(plan.ctx, block, width),
        dw_qkv.reshape(plan.devices, plan.rows, plan.wide),
        dw_mix,
        dw_in,
    )

    normed_grad = jnp.sum(dn.astype(F32), axis=0).reshape(local, width)
    inverse_one = lax.rsqrt(jnp.mean(x * x, axis=-1, keepdims=True) + EPSILON)
    scaled = normed_grad * gain_one
    input_grad = (
        middle_grad
        + inverse_one * scaled
        - x * inverse_one**3 * jnp.mean(scaled * x, axis=-1, keepdims=True)
    )
    input_grad = input_grad.astype(BF16).reshape(2, block, width)
    r_qkv = r_qkv.astype(F32).reshape(plan.dp * HALVES, quad, plan.rows, plan.wide)
    r_qkv = jnp.sum(r_qkv, axis=0)
    attn_in_grad = unpack_qkv(plan, r_qkv)
    small = jnp.sum(r_qkv[:, :, plan.qkv_cols :], axis=0)
    attn_out_grad = jnp.sum(r_mix.astype(F32), axis=0)
    dense_in_grad, expert_in_grad = unpack_in(plan, r_in)
    return (
        by_half(half, activations[0], swap(activations[1]), 0)[:, None],
        by_half(half, input_grad[0], swap(input_grad[1]), 0)[:, None],
        small[:, 0],
        attn_in_grad,
        attn_out_grad,
        small[:, 1],
        small[:, 2 : 2 + experts],
        dense_in_grad,
        dw_out[0],
        expert_in_grad,
        jnp.transpose(dw_out[1:], (1, 0, 2)),
    )


def solution(mesh):
    rows = P(("dp", "ctx"))
    matrix = P(("dp", "ctx"), None)
    cube = P(("dp", "ctx"), None, None)
    slots = P(None, "dp", "ctx", None)
    in_specs = (
        slots,
        P(None, "dp"),
        slots,
        slots,
        rows,
        matrix,
        matrix,
        rows,
        matrix,
        matrix,
        matrix,
        cube,
        cube,
    )
    out_specs = (
        slots,
        slots,
        rows,
        matrix,
        matrix,
        rows,
        matrix,
        matrix,
        matrix,
        cube,
        cube,
    )
    return jax.shard_map(shards, mesh=mesh, in_specs=in_specs, out_specs=out_specs, check_vma=False)
```

time: 2430 us -> 565 us (0.23)
  waiting for transfers between devices: 1580 us -> 30.5 us
  matrix products: 491 us -> 7.71 us
  Pallas kernels: 0 us -> 411 us
  blocking collectives: 149 us -> 0 us
  local copies, waits for them, and re-layouts: 114 us -> 49.7 us
  other arithmetic: 68.5 us -> 27.7 us
    reduce_scatter x10 -> x0, waiting for transfers between devices: 1190 us -> none  [the longest x1 436 us: shards(): lax.psum_scatter(running[7], ('dp', 'ctx'), scatter_dimension=0, tiled=True)]
    dot_general x246 -> x6, matrix products: 491 us -> 7.71 us  [the longest x2 3.12 us: nn(): lax.dot_general(left, right, (((1,), (0,)), ((), ())), preferred_element_...]
    pallas_call x0 -> x11, Pallas kernels: none -> 411 us  [the longest x1 77.5 us: collect(): pl.pallas_call(functools.partial(collect_kernel, plan), out_shape=(jax.Sh...]
    all_gather x10 -> x1, waiting for transfers between devices: 389 us -> 0.01 us  [shards(): w_mix = lax.all_gather(attn_out, ('dp', 'ctx'), axis=0, tiled=True)]
    unnamed x2 -> x0, blocking collectives: 82.4 us -> none
    all_gather x1 -> x0, blocking collectives: 66.5 us -> none  [shards(): lax.all_gather(router, ('dp', 'ctx'), axis=0, tiled=True)]
    unnamed x373 -> x44, local copies, waits for them, and re-layouts: 44.1 us -> 5.77 us
    lt x48 -> x0, other arithmetic: 30.9 us -> none  [head_scores(): key_places[None, None, :] < seq_lengths[:, None, None]]
  transfers between devices with their start and end apart: 20 -> 9, of which waited for: 16 -> 1; matrix products, arithmetic and copies ran while one was open for 20% -> 12% of each run, Pallas kernels for 0% -> 32%
where the time goes in v1:
time: 565 us; the launch traced here: 558 us
  Pallas kernels  411 us (73%)
  local copies, waits for them, and re-layouts  49.7 us (9%)
  waiting for transfers between devices  30.5 us (5%)
  other arithmetic  27.7 us (5%)
  starting transfers between devices  16.5 us (3%)
  between operations  14.9 us (3%)
  matrix products  7.71 us (1%)
    pallas_call x1, Pallas kernels, collect(): pl.pallas_call(functools.partial(collect_kernel, plan), out_shape=(jax.Sh...  77.5 us
    pallas_call x2, Pallas kernels, gather(): pl.pallas_call(functools.partial(gather_kernel, plan), out_shape=jax.Shap...  71.6 us
    pallas_call x1, Pallas kernels, spread(): pl.pallas_call(functools.partial(spread_kernel, plan), out_shape=(jax.Sha...  67.6 us
    pallas_call x2, Pallas kernels, reduce(): pl.pallas_call(functools.partial(reduce_kernel, plan), out_shape=jax.Shap...  66.4 us
    pallas_call x1, Pallas kernels, ffn(): pl.pallas_call(functools.partial(ffn_kernel, plan, members), grid=(plan.g...  52 us
    pallas_call x1, Pallas kernels, to_owners(): pl.pallas_call(functools.partial(to_owners_kernel, plan), out_shape=jax.S...  31.2 us
    ppermute x8, waiting for transfers between devices, swap(): return lax.ppermute(value, 'ctx', across)  29.8 us
    pallas_call x1, Pallas kernels, attend_back(): pl.pallas_call(functools.partial(attend_back_kernel, plan), out_shape=(ja...  17.7 us
  transfers between devices with their start and end apart: 9, of which 1 were waited for; matrix products, arithmetic and copies ran while one was open for 12% of the time, Pallas kernels for 32%

profile of v1, /device:TPU:0, one launch (start us, length us, event | category | flops | bytes accessed | tf_op | source)
XLA Modules:
  0.0 558.0 jit_solution(8561466443292612218)
XLA Ops:
  8.7 4.1 collective-permute-start
  12.8 1.7 dynamic-slice_bitcast_fusion.1
  15.6 1.7 fusion.14
  17.3 2.9 collective-permute-start.3
  21.8 3.2 concatenate.74
  26.3 3.1 maximum_bitcast_fusion
  29.5 2.1 reshape.464.win
  32.4 67.6 %spread.1 = (bf16[8,128,768]{2,1,0:T(8,128)(2,1)}, bf16[32,24,640]{2,1,0:T(8,128)(2,1)}, bf16[16,24,1280]{2,1,0:T(8,128)(2,1)}) custom-call(bf16[2,128,768]{2,1,0:T(8,128)(2,1)} %bitcast.184, bf16[4,24,640]{2,1,0:T(8,128)(2,1)} %pad_maximum_fusion.4.wq, bf16[16,24,1280]{2,1,0:T(8,128)(2,1)} %reshape.464.win), custom_call_target="tpu_custom_call" | custom-call | tf_op jit(solution)/shard_map/spread/pallas_call | solution.py:149
  99.9 2.4 collective-permute-start.2
  106.9 12.0 %attend.1 = (bf16[1024,192]{1,0:T(8,128)(2,1)}, bf16[1024,768]{1,0:T(8,128)(2,1)}, bf16[1024,384]{1,0:T(8,128)(2,1)}, bf16[1024,192]{1,0:T(8,128)(2,1)}, f32[3,1024,1]{2,1,0:T(8,128)}) custom-call(s32[1]{0:T(128)} %bitcast.8.length_ref, bf16[1024,768]{1,0:T(8,128)(2,1)} %bitcast.157, f32[1,768]{1,0:T(1,128)} %reshape.483.gain, bf16[768,640]{1,0:T(8,128)(2,1)} %bitcast.161, ...), custom_call_target="tpu_custom_call" | custom-call | tf_op jit(solution)/shard_map/attend/pallas_call | solution.py:613
  119.0 31.2 %to_owners.1 = bf16[4,2,128,192]{3,2,1,0:T(8,128)(2,1)} custom-call(bf16[8,128,192]{2,1,0:T(8,128)(2,1)} %bitcast.183), custom_call_target="tpu_custom_call" | custom-call | tf_op jit(solution)/shard_map/to_owners/pallas_call | solution.py:230
  153.3 35.1 %gather.3.gy = bf16[16,256,768]{2,1,0:T(8,128)(2,1)} custom-call(bf16[256,768]{1,0:T(8,128)(2,1)} %bitcast_multiply_fusion.2.src), custom_call_target="tpu_custom_call" | custom-call | tf_op jit(solution)/shard_map/gather/pallas_call | solution.py:426
  190.9 3.1 maximum_select_fusion
  194.0 1.9 multiply_reduce_fusion.4
  198.9 36.5 %gather.2.n2x = bf16[16,272,768]{2,1,0:T(8,128)(2,1)} custom-call(bf16[272,768]{1,0:T(8,128)(2,1)} %fusion.9.src), custom_call_target="tpu_custom_call" | custom-call | tf_op jit(solution)/shard_map/gather/pallas_call | solution.py:426
  235.4 52.0 %ffn.1 = (bf16[16,256,768]{2,1,0:T(8,128)(2,1)}, bf16[16,272,768]{2,1,0:T(8,128)(2,1)}, f32[768,1280]{1,0:T(8,128)}, f32[640,768]{1,0:T(8,128)}) custom-call(bf16[16,272,768]{2,1,0:T(8,128)(2,1)} %gather.2.n2x, bf16[16,256,768]{2,1,0:T(8,128)(2,1)} %gather.3.gy, bf16[768,1280]{1,0:T(8,128)(2,1)} %bitcast.159, bf16[640,768]{1,0:T(8,128)(2,1)} %bitcast.168, ...), custom_call_target="tpu_custom_call" | custom-call | tf_op jit(solution)/shard_map/ffn/pallas_call | solution.py:740
  287.4 34.7 %reduce.14 = f32[272,768]{1,0:T(8,128)} custom-call(bf16[16,272,768]{2,1,0:T(8,128)(2,1)} %get-tuple-element.35.src), custom_call_target="tpu_custom_call" | custom-call | tf_op jit(solution)/shard_map/reduce/pallas_call | solution.py:528
  323.7 1.8 multiply_reduce_fusion.1
  325.5 31.7 %reduce.13 = f32[256,768]{1,0:T(8,128)} custom-call(bf16[16,256,768]{2,1,0:T(8,128)(2,1)} %get-tuple-element.34.src), custom_call_target="tpu_custom_call" | custom-call | tf_op jit(solution)/shard_map/reduce/pallas_call | solution.py:528
  357.3 2.0 fusion.8
  359.3 2.5 collective-permute-start.7
  366.7 14.9 %to_slots.1 = bf16[8,128,192]{2,1,0:T(8,128)(2,1)} custom-call(bf16[4,2,128,192]{3,2,1,0:T(8,128)(2,1)} %bitcast.176), custom_call_target="tpu_custom_call" | custom-call | tf_op jit(solution)/shard_map/to_slots/pallas_call | solution.py:193
  381.7 2.7 fusion.1
  384.3 17.7 %attend_back.1 = (bf16[1024,768]{1,0:T(8,128)(2,1)}, f32[768,640]{1,0:T(8,128)}, f32[1,768]{1,0:T(1,128)}) custom-call(s32[1]{0:T(128)} %bitcast.8.length_ref, bf16[1024,768]{1,0:T(8,128)(2,1)} %bitcast.158, bf16[768,640]{1,0:T(8,128)(2,1)} %bitcast.164, f32[1024,128]{1,0:T(8,128)} %constant.88.clone.cosine, f32[1024,128]{1,0:T(8,128)} %constant.89.clone.sine, ...), custom_call_target="tpu_custom_call" | custom-call | tf_op jit(solution)/shard_map/attend_back/pallas_call | solution.py:678
  404.7 3.0 collective-permute-start.5
  413.0 29.8 %collective-permute-done.5 = bf16[4,4,24,1280]{3,2,1,0:T(8,128)(2,1)S(1)} collective-permute-done((bf16[4,4,24,1280]{3,2,1,0:T(8,128)(2,1)}, bf16[4,4,24,1280]{3,2,1,0:T(8,128)(2,1)S(1)}, u32[]{:S(2)}, u32[]{:S(2)}) %collective-permute-start.5) | collective-permute-done | bytes 983072 | tf_op jit(solution)/shard_map/ppermute | solution.py:859
  444.0 77.5 %collect.1 = (bf16[4,2,128,768]{3,2,1,0:T(8,128)(2,1)}, bf16[32,24,640]{2,1,0:T(8,128)(2,1)}, bf16[32,24,768]{2,1,0:T(8,128)(2,1)}, bf16[16,24,1280]{2,1,0:T(8,128)(2,1)}) custom-call(bf16[8,128,768]{2,1,0:T(8,128)(2,1)} %bitcast.177, bf16[32,24,640]{2,1,0:T(8,128)(2,1)} %pad_maximum_fusion.dwq, bf16[32,24,768]{2,1,0:T(8,128)(2,1)} %bitcast.165, ...), custom_call_target="tpu_custom_call" | custom-call | tf_op jit(solution)/shard_map/collect/pallas_call | solution.py:281
  526.5 5.0 reshape.490
  531.5 6.5 %copy.164 = f32[4,4,24,2,5,2,64]{6,1,5,0,3,2,4:T(4,128)} copy(f32[4,4,24,2,5,2,64]{6,5,4,3,2,1,0:T(2,128)} %reshape.490) | data formatting | bytes 3932160 | tf_op jit(solution)/shard_map/convert_element_type | solution.py:830
  538.0 4.1 reshape.489
  546.1 2.2 copy.142
  549.1 1.8 maximum_select_fusion.3
  (145 shorter events, 44.5 us)
Async XLA Ops:
  7.2 96.4 %copy-start = (s32[2,1]{0,1:T(1,128)S(1)}, s32[2,1]{0,1:T(1,128)}, u32[]{:S(2)}) copy-start(s32[2,1]{0,1:T(1,128)} %param.17) | copy-start | bytes 28
  7.2 13.0 %copy-start.11 = (bf16[24,2304]{1,0:T(8,128)(2,1)S(1)}, bf16[24,2304]{1,0:T(8,128)(2,1)}, u32[]{:S(2)}) copy-start(bf16[24,2304]{1,0:T(8,128)(2,1)} %param.21) | copy-start | bytes 331780
  7.2 186.8 %all-gather.2.cloned.1.call-start = ((), (), s32[]{:S(2)}) async-start(), calls=%async_computation | async-start | bytes 1216512 | tf_op jit(solution)/shard_map/all_gather | solution.py:874
  8.7 11.9 %copy-start.16 = (bf16[24,4]{0,1:T(4,128)(2,1)S(1)}, bf16[24,4]{0,1:T(4,128)(2,1)}, u32[]{:S(2)}) copy-start(bf16[24,4]{0,1:T(4,128)(2,1)} %param.24) | copy-start | bytes 580
  8.7 11.9 %copy-start.17 = (bf16[24]{0:T(256)(128)(2,1)S(1)}, bf16[24]{0:T(256)(128)(2,1)}, u32[]{:S(2)}) copy-start(bf16[24]{0:T(256)(128)(2,1)} %param.23) | copy-start | bytes 148
  8.7 11.9 %copy-start.18 = (bf16[24]{0:T(256)(128)(2,1)S(1)}, bf16[24]{0:T(256)(128)(2,1)}, u32[]{:S(2)}) copy-start(bf16[24]{0:T(256)(128)(2,1)} %param.20) | copy-start | bytes 148
  8.7 142.8 %collective-permute-start = (s32[128,2]{0,1:T(2,128)S(1)}, s32[128,2]{0,1:T(2,128)S(1)}, u32[]{:S(2)}, u32[]{:S(2)}) collective-permute-start(s32[128,2]{0,1:T(2,128)S(1)} %get-tuple-element.116), channel_id=1, source_target_pairs={{0,4},{1,5},{2,6},{3,7},{4,0},{5,1},{6,2},{7,3},{8,12},{9,13},{10,... | collective-permute-start | bytes 3080 | tf_op jit(solution)/shard_map/ppermute | solution.py:859
  14.5 6.6 %copy-start.10 = (bf16[24,4096]{1,0:T(8,128)(2,1)S(1)}, bf16[24,4096]{1,0:T(8,128)(2,1)}, u32[]{:S(2)}) copy-start(bf16[24,4096]{1,0:T(8,128)(2,1)} %param.25) | copy-start | bytes 589828
  14.5 137.0 %collective-permute-start.1 = (bf16[128,768]{1,0:T(8,128)(2,1)}, bf16[128,768]{1,0:T(8,128)(2,1)}, u32[]{:S(2)}, u32[]{:S(2)}) collective-permute-start(bf16[128,768]{1,0:T(8,128)(2,1)} %get-tuple-element.114), channel_id=1, source_target_pairs={{0,4},{1,5},{2,6},{3,7},{4,0},{5,1},{6,2},{7,3},{8,12},{9,13},{10,... | collective-permute-start | bytes 589832 | tf_op jit(solution)/shard_map/ppermute | solution.py:859
  17.3 171.1 %collective-permute-start.3 = (bf16[5,64,768]{2,1,0:T(8,128)(2,1)}, bf16[5,64,768]{2,1,0:T(8,128)(2,1)}, u32[]{:S(2)}, u32[]{:S(2)}) collective-permute-start(bf16[5,64,768]{2,1,0:T(8,128)(2,1)} %get-tuple-element.108), channel_id=1, source_target_pairs={{0,4},{1,5},{2,6},{3,7},{4,0},{5,1},{6,2},{7,3},{8,12},{9,13},{10,... | collective-permute-start | bytes 1474568 | tf_op jit(solution)/shard_map/ppermute | solution.py:859
  99.9 91.0 %collective-permute-start.2 = (bf16[16,24,1280]{2,1,0:T(8,128)(2,1)}, bf16[16,24,1280]{2,1,0:T(8,128)(2,1)}, u32[]{:S(2)}, u32[]{:S(2)}) collective-permute-start(bf16[16,24,1280]{2,1,0:T(8,128)(2,1)} %get-tuple-element.33), channel_id=1, source_target_pairs={{0,4},{1,5},{2,6},{3,7},{4,0},{5,1},{6,2},{7,3},{8,12},{9,13},{10,... | collective-permute-start | bytes 2949128 | tf_op jit(solution)/shard_map/ppermute | solution.py:859
  104.8 47.7 %copy-start.14 = (bf16[256]{0:T(256)(128)(2,1)}, bf16[256]{0:T(256)(128)(2,1)S(1)}, u32[]{:S(2)}) copy-start(bf16[256]{0:T(256)(128)(2,1)S(1)} %fusion.28) | copy-start | bytes 1540
  188.5 2.5 copy-start.9
  325.5 36.3 %copy-start.13 = (f32[256]{0:T(256)S(1)}, f32[256]{0:T(256)}, u32[]{:S(2)}) copy-start(f32[256]{0:T(256)} %get-tuple-element.117) | copy-start | bytes 3076
  325.5 36.3 %copy-start.15 = (bf16[256]{0:T(256)(128)(2,1)S(1)}, bf16[256]{0:T(256)(128)(2,1)}, u32[]{:S(2)}) copy-start(bf16[256]{0:T(256)(128)(2,1)} %copy-done.14) | copy-start | bytes 1540
  359.3 50.2 %collective-permute-start.7 = (bf16[5,64,768]{2,1,0:T(8,128)(2,1)}, bf16[5,64,768]{2,1,0:T(8,128)(2,1)}, u32[]{:S(2)}, u32[]{:S(2)}) collective-permute-start(bf16[5,64,768]{2,1,0:T(8,128)(2,1)} %fusion.8), channel_id=1, source_target_pairs={{0,4},{1,5},{2,6},{3,7},{4,0},{5,1},{6,2},{7,3},{8,12},{9,13},{10,... | collective-permute-start | bytes 1474568 | tf_op jit(solution)/shard_map/ppermute | solution.py:859
  363.3 1.6 copy-start.3
  381.6 27.1 %collective-permute-start.4 = (bf16[128,768]{1,0:T(8,128)(2,1)S(1)}, bf16[128,768]{1,0:T(8,128)(2,1)S(1)}, u32[]{:S(2)}, u32[]{:S(2)}) collective-permute-start(bf16[128,768]{1,0:T(8,128)(2,1)S(1)} %get-tuple-element.112), channel_id=1, source_target_pairs={{0,4},{1,5},{2,6},{3,7},{4,0},{5,1},{6,2},{7,3},{8,12},{9,13},{10,... | collective-permute-start | bytes 589832 | tf_op jit(solution)/shard_map/ppermute | solution.py:859
  384.3 18.4 %copy-start.12 = (bf16[768,4]{0,1:T(4,128)(2,1)S(1)}, bf16[768,4]{0,1:T(4,128)(2,1)}, u32[]{:S(2)}) copy-start(bf16[768,4]{0,1:T(4,128)(2,1)} %convolution_convert_fusion.2) | copy-start | bytes 18436
  404.7 4.9 copy-start.8
  404.7 38.1 %collective-permute-start.5 = (bf16[4,4,24,1280]{3,2,1,0:T(8,128)(2,1)}, bf16[4,4,24,1280]{3,2,1,0:T(8,128)(2,1)S(1)}, u32[]{:S(2)}, u32[]{:S(2)}) collective-permute-start(bf16[4,4,24,1280]{3,2,1,0:T(8,128)(2,1)} %fusion.1), channel_id=1, source_target_pairs={{0,4},{1,5},{2,6},{3,7},{4,0},{5,1},{6,2},{7,3},{8,12},{9,13},{10,... | collective-permute-start | bytes 2949128 | tf_op jit(solution)/shard_map/ppermute | solution.py:859
  409.5 33.2 %copy-start.4 = (f32[768,1280]{1,0:T(8,128)S(1)}, f32[768,1280]{1,0:T(8,128)}, u32[]{:S(2)}) copy-start(f32[768,1280]{1,0:T(8,128)} %get-tuple-element.43) | copy-start | bytes 11796484
  521.5 1.7 copy-start.5
  522.9 0.7 copy-start.6
  523.6 0.9 slice-start.1
  523.7 1.0 slice-start.2
  524.9 24.2 %collective-permute-start.6 = (bf16[128,768]{1,0:T(8,128)(2,1)S(1)}, bf16[128,768]{1,0:T(8,128)(2,1)}, u32[]{:S(2)}, u32[]{:S(2)}) collective-permute-start(bf16[128,768]{1,0:T(8,128)(2,1)S(1)} %get-tuple-element.110), channel_id=1, source_target_pairs={{0,4},{1,5},{2,6},{3,7},{4,0},{5,1},{6,2},{7,3},{8,12},{9,13},{10,... | collective-permute-start | bytes 589832 | tf_op jit(solution)/shard_map/ppermute | solution.py:859
  542.1 1.9 copy-start.2
  544.7 1.4 slice-start
  544.9 6.0 %copy-start.1 = (s32[2,1]{0,1:T(1,128)S(1)}, s32[2,1]{0,1:T(1,128)}, u32[]{:S(2)}) copy-start(s32[2,1]{0,1:T(1,128)} %param.17) | copy-start | bytes 28
  546.1 2.2 copy-start.7
Sparse Core Ops, SparseCore 0:
  11.0 73.1 all-gather.1

commit v2 on v1

--- a/solution.py
+++ b/solution.py
@@ -764,6 +764,258 @@
     )(n2x, gy, w_in, w_out, pick)
 
 
+STEP_ORDER = ((0, 0, 0), (0, 1, 0), (0, 1, 1), (1, 1, 0), (1, 1, 1), (1, 0, 1), (1, 0, 0), (0, 0, 1))
+FUSED_GATHER = (("high", "low", "y"), ("y", "low", "high"))
+FUSED_REDUCE = (("low", "high", "y"), ("y", "high", "low"))
+
+
+def named(offset):
+    return dict(zip(("high", "low", "y"), offset))
+
+
+def sum_plan(order):
+    taken = {offset: step for step, offset in enumerate(STEP_ORDER)}
+    names = ("high", "low", "y")
+    rows, ready = [], {}
+    for phase in range(4):
+        for offset in STEP_ORDER:
+            at = named(offset)
+            if any(at[axis] for axis in order[:phase]) or (phase < 3 and not at[order[phase]]):
+                continue
+            if phase == 3 and any(offset):
+                continue
+            feeds = [
+                tuple(1 if name == axis else at[name] for name in names) for axis in order[:phase]
+            ]
+            when = max([taken[offset] + 1] + [ready[feed] for feed in feeds])
+            rows.append((when, phase, offset, order[phase] if phase < 3 else None, feeds))
+            ready[offset] = when + 2
+    rows.sort(key=lambda row: (row[0], row[1]))
+    return rows
+
+
+def fused_kernel(plan, n2x, gy, w_in, w_out, pick, total, dw_in, dw_out, n2all, gybuf, acc, away, work, core_buf, bufs, gy_sem, g_send, g_recv, gc_send, gc_recv, c_send, c_recv, r_send, r_recv):
+    grid = Grid(plan)
+    at = grid.here()
+    local, width, hidden = plan.local, plan.width, plan.hidden_pad
+    steps = len(STEP_ORDER)
+    partner = grid.device(grid.moved(at, "core", 1))
+    here = grid.device(at)
+    colors = range(2)
+
+    def absolute(offset):
+        where = dict(at)
+        for axis, step in named(offset).items():
+            if step:
+                where = grid.moved(where, axis, step)
+        return where
+
+    def slot_of(offset):
+        return grid.slot(named(offset))
+
+    send_index = [{}, {}]
+    for color in colors:
+        for offset in STEP_ORDER:
+            order = FUSED_GATHER[color]
+            reached = named(offset)
+            level = max([i + 1 for i, axis in enumerate(order) if reached[axis]], default=0)
+            for axis in order[level:]:
+                send_index[color][(offset, axis)] = len(send_index[color])
+
+    def pass_on(color, offset):
+        order = FUSED_GATHER[color]
+        reached = named(offset)
+        level = max([i + 1 for i, axis in enumerate(order) if reached[axis]], default=0)
+        where = absolute(offset)
+        block = grid.block(where)
+        slot = slot_of(offset)
+        if level:
+            remote(n2all.at[block], n2all.at[block], g_send.at[0], g_recv.at[slot], here).wait_recv()
+        source = n2all.at[block] if level else n2x
+        remote(source, n2all.at[block], gc_send.at[slot], gc_recv.at[slot], partner).start()
+        for axis in order[level:]:
+            seen = grid.slot({**reached, axis: 1})
+            remote(
+                source,
+                n2all.at[block],
+                g_send.at[send_index[color][(offset, axis)]],
+                g_recv.at[seen],
+                grid.device(grid.moved(at, axis, 1)),
+            ).start()
+
+    plans = [sum_plan(order) for order in FUSED_REDUCE]
+    buf_index = [{row[2]: i for i, row in enumerate(rows) if row[3]} for rows in plans]
+
+    def add_up(color, row):
+        _, _, offset, axis, feeds = row
+        slot = slot_of(offset)
+        remote(away.at[0], core_buf.at[slot], c_send.at[0], c_recv.at[slot], here).wait_recv()
+        for feed in feeds:
+            index = buf_index[color][feed]
+            remote(away.at[0], bufs.at[index], r_send.at[0], r_recv.at[index], here).wait_recv()
+        rows = work.shape[1]
+        chunk = 48
+
+        @pl.loop(0, rows // chunk)
+        def _(i):
+            span = pl.ds(pl.multiple_of(i * chunk, 16), chunk)
+            value = work[slot, span].astype(F32) + core_buf[slot, span].astype(F32)
+            for feed in feeds:
+                value = value + bufs[buf_index[color][feed], span].astype(F32)
+            if axis is None:
+                total[span] = value
+            else:
+                work[slot, span] = value.astype(BF16)
+
+        if axis is not None:
+            index = buf_index[color][offset]
+            remote(
+                work.at[slot],
+                bufs.at[index],
+                r_send.at[index],
+                r_recv.at[index],
+                grid.device(grid.moved(at, axis, 1)),
+            ).start()
+
+    def pump(step):
+        def run(color):
+            for offset in STEP_ORDER:
+                if 0 < step == sum(offset):
+                    pass_on(color, offset)
+            for row in plans[color]:
+                if row[0] == step or (step == steps and row[0] > steps):
+                    add_up(color, row)
+
+        for color in colors:
+            pl.when(at["core"] == color)(functools.partial(run, color))
+
+    def bit(step, index):
+        value = 0
+        for i, offset in enumerate(STEP_ORDER):
+            if offset[index]:
+                value = value + jnp.where(step == i, 1, 0)
+        return value
+
+    def blocks_of(step):
+        where = dict(at)
+        offsets = {}
+        for index, axis in enumerate(("high", "low", "y")):
+            offsets[axis] = bit(step, index)
+            where[axis] = lax.rem(at[axis] + offsets[axis], 2)
+        mine = grid.block(where)
+        other = grid.block(grid.moved(where, "core", 1))
+        return mine, other, grid.slot(offsets)
+
+    def gy_loads(step, turn):
+        mine, other, _ = blocks_of(step)
+        return [
+            pltpu.make_async_copy(gy.at[mine], gybuf.at[turn, 0], gy_sem.at[turn, 0]),
+            pltpu.make_async_copy(gy.at[other], gybuf.at[turn, 1], gy_sem.at[turn, 1]),
+        ]
+
+    for load in gy_loads(0, 0):
+        load.start()
+    meet(grid.peers(at))
+    for color in colors:
+        pl.when(at["core"] == color)(functools.partial(pass_on, color, STEP_ORDER[0]))
+    n2all[pl.ds(grid.block(at), 1)] = n2x[...][None]
+    acc[...] = jnp.zeros_like(acc)
+    dw_out[...] = jnp.zeros_like(dw_out)
+
+    @pl.loop(0, steps)
+    def _(step):
+        for i in range(1, steps):
+            pl.when(step == i)(functools.partial(pump, i))
+        mine, other, slot = blocks_of(step)
+        turn = lax.rem(step, 2)
+
+        @pl.when(step + 1 < steps)
+        def _():
+            for load in gy_loads(step + 1, 1 - turn):
+                load.start()
+
+        remote(n2x, n2all.at[other], gc_send.at[0], gc_recv.at[slot], here).wait_recv()
+        for load in gy_loads(step, turn):
+            load.wait()
+        pair = (mine, other)
+        normed = jnp.concatenate([n2all[b, :local] for b in pair], axis=0)
+        upstream = gybuf[turn].reshape(2 * local, width)
+        mixing = jnp.concatenate([tn(n2all[b, local:, :local], pick[...]) for b in pair], axis=0)
+        pre = nn(normed, w_in[...])
+        gate, up = pre[:, :hidden], pre[:, hidden:]
+        sigmoid = jax.nn.sigmoid(gate)
+        silu = gate * sigmoid
+        act = (silu * up).astype(BF16).astype(F32)
+        act_mixed = (act * mixing).astype(BF16)
+        out = nn(act_mixed, w_out[...]).astype(BF16)
+        act_grad = nt(upstream, w_out[...])
+        choice = nt(pick[...], (act * act_grad).astype(BF16)).astype(BF16)
+        act_grad = act_grad * mixing
+        gate_grad = act_grad * up * sigmoid * (1.0 + gate * (1.0 - sigmoid))
+        pre_grad = jnp.concatenate([gate_grad, act_grad * silu], axis=-1).astype(BF16)
+        n2g = nt(pre_grad, w_in[...]).astype(BF16)
+
+        @pl.when(step >= 2)
+        def _():
+            remote(away.at[turn], core_buf.at[0], c_send.at[turn], c_recv.at[0], partner).wait_send()
+
+        pad = jnp.zeros((MIX_ROWS, width - local), BF16)
+        for i, (ref, index) in enumerate(((work, slot), (away, turn))):
+            span = slice(i * local, (i + 1) * local)
+            ref[index, :local] = n2g[span]
+            ref[index, local : local + MIX_ROWS] = jnp.concatenate([choice[:, span], pad], axis=-1)
+            ref[index, local + MIX_ROWS :] = out[span]
+        remote(away.at[turn], core_buf.at[slot], c_send.at[turn], c_recv.at[slot], partner).start()
+        acc[...] += tn(normed, pre_grad)
+        dw_out[...] += tn(act_mixed, upstream)
+
+    pump(steps)
+    dw_in[...] = acc[...].astype(BF16)
+    for turn in range(2):
+        remote(away.at[turn], core_buf.at[0], c_send.at[turn], c_recv.at[0], partner).wait_send()
+    for slot in range(steps):
+        remote(n2x, n2all.at[0], gc_send.at[slot], gc_recv.at[0], partner).wait_send()
+    for index in range(steps - 1):
+        remote(n2x, n2all.at[0], g_send.at[index], g_recv.at[0], partner).wait_send()
+        remote(work.at[0], bufs.at[index], r_send.at[index], r_recv.at[0], partner).wait_send()
+
+
+def fused(plan, n2x, gy, w_in, w_out, pick, collective_id):
+    local, width, hidden = plan.local, plan.width, plan.hidden_pad
+    steps = len(STEP_ORDER)
+    rows = 2 * local + MIX_ROWS
+    return pl.pallas_call(
+        functools.partial(fused_kernel, plan),
+        out_shape=(
+            jax.ShapeDtypeStruct((rows, width), F32),
+            jax.ShapeDtypeStruct((width, 2 * hidden), BF16),
+            jax.ShapeDtypeStruct((hidden, width), F32),
+        ),
+        in_specs=[VMEM, HBM, VMEM, VMEM, VMEM],
+        out_specs=(VMEM,) * 3,
+        scratch_shapes=[
+            pltpu.VMEM((plan.group, local + MIX_ROWS, width), BF16),
+            pltpu.VMEM((2, 2, local, width), BF16),
+            pltpu.VMEM((width, 2 * hidden), F32),
+            pltpu.VMEM((2, rows, width), BF16),
+            pltpu.VMEM((steps, rows, width), BF16),
+            pltpu.VMEM((steps, rows, width), BF16),
+            pltpu.VMEM((steps - 1, rows, width), BF16),
+            DMA((2, 2)),
+            DMA((steps - 1,)),
+            DMA((steps,)),
+            DMA((steps,)),
+            DMA((steps,)),
+            DMA((2,)),
+            DMA((steps,)),
+            DMA((steps - 1,)),
+            DMA((steps - 1,)),
+        ],
+        compiler_params=params(collective_id),
+        name="fused",
+    )(n2x, gy, w_in, w_out, pick)
+
+
 def by_half(half, mine, far, axis):
     return jnp.where(
         half == 0, jnp.stack([mine, far], axis), jnp.stack([far, mine], axis)
@@ -919,7 +1171,7 @@
         ]
     )
     mix_rows = jnp.pad(mix_rows, ((0, 0), (0, width - local)))
-    n2x = gather(plan, jnp.concatenate([normed_two, mix_rows]), 3)
+    n2x = jnp.concatenate([normed_two, mix_rows])
 
     starts = jnp.stack([ctx, (1 - half) * quad + member]) * block
     slot = (starts[:, None] + jnp.arange(block, dtype=jnp.int32)[None]).reshape(local)
@@ -932,9 +1184,14 @@
     w_in = w_in.reshape(width, 2 * plan.hidden_pad)
     w_out = by_half(half, out_own, out_far, 1).reshape(plan.hidden, width)
     w_out = jnp.pad(w_out, ((0, plan.hidden_pad - plan.hidden), (0, 0)))
-    out_part, n2g_part, dw_in, dw_out = ffn(plan, n2x, gy, w_in, w_out, pick_table(plan))
-    n2g_sum = reduce(plan, n2g_part, 5)
-    out_sum = reduce(plan, out_part, 7)
+    if plan.dp == 4 and quad == 4:
+        sums, dw_in, dw_out = fused(plan, n2x, gy, w_in, w_out, pick_table(plan), 3)
+        n2g_sum, out_sum = sums[: local + MIX_ROWS], sums[local + MIX_ROWS :]
+    else:
+        n2x = gather(plan, n2x, 3)
+        out_part, n2g_part, dw_in, dw_out = ffn(plan, n2x, gy, w_in, w_out, pick_table(plan))
+        n2g_sum = reduce(plan, n2g_part, 5)
+        out_sum = reduce(plan, out_part, 7)
     activations = (middle + out_sum).astype(BF16).reshape(2, block, width)
 
     dw_out = dw_out[: plan.hidden].reshape(plan.branches, HALVES, plan.own_hidden, width)
@@ -942,7 +1199,7 @@
     dw_out = pick_mine(dw_out) + swap(pick_far(dw_out).astype(BF16)).astype(F32)
     dw_in = dw_in.reshape(plan.dp, HALVES, quad, plan.rows, 2 * plan.hidden_pad)
     dw_in = jnp.moveaxis(dw_in, 1, 0)
-    dw_in = pick_mine(dw_in) + swap(pick_far(dw_in).astype(BF16)).astype(F32)
+    dw_in = pick_mine(dw_in).astype(F32) + swap(pick_far(dw_in).astype(BF16)).astype(F32)
     dw_in = dw_in.astype(BF16).reshape(plan.group, plan.rows, 2 * plan.hidden_pad)
 
     normed_two_grad = n2g_sum[:local]

time: 565 us -> 528 us (0.935)
  Pallas kernels: 411 us -> 377 us
    pallas_call x2 -> x1, Pallas kernels: 71.6 us -> 35.2 us  [gather(): pl.pallas_call(functools.partial(gather_kernel, plan), out_shape=jax.Shap...]
    pallas_call x3 -> x1, Pallas kernels: 118 us -> 112 us  [fused(): pl.pallas_call(functools.partial(fused_kernel, plan), out_shape=(jax.Shap...]
  transfers between devices with their start and end apart: 9 -> 9, of which waited for: 1 -> 1; matrix products, arithmetic and copies ran while one was open for 12% -> 13% of each run, Pallas kernels for 32% -> 35%
where the time goes in v2:
time: 528 us; the launch traced here: 520 us
  Pallas kernels  377 us (71%)
  local copies, waits for them, and re-layouts  48.8 us (9%)
  waiting for transfers between devices  29.1 us (6%)
  other arithmetic  27 us (5%)
  starting transfers between devices  16.6 us (3%)
  between operations  15.1 us (3%)
  matrix products  7.15 us (1%)
    pallas_call x1, Pallas kernels, fused(): pl.pallas_call(functools.partial(fused_kernel, plan), out_shape=(jax.Shap...  112 us
    pallas_call x1, Pallas kernels, collect(): pl.pallas_call(functools.partial(collect_kernel, plan), out_shape=(jax.Sh...  82.2 us
    pallas_call x1, Pallas kernels, spread(): pl.pallas_call(functools.partial(spread_kernel, plan), out_shape=(jax.Sha...  67.6 us
    pallas_call x1, Pallas kernels, gather(): pl.pallas_call(functools.partial(gather_kernel, plan), out_shape=jax.Shap...  35.2 us
    pallas_call x1, Pallas kernels, to_owners(): pl.pallas_call(functools.partial(to_owners_kernel, plan), out_shape=jax.S...  31.2 us
    ppermute x8, waiting for transfers between devices, swap(): return lax.ppermute(value, 'ctx', across)  28.4 us
    pallas_call x1, Pallas kernels, to_slots(): pl.pallas_call(functools.partial(to_slots_kernel, plan), out_shape=jax.Sh...  18.9 us
    pallas_call x1, Pallas kernels, attend_back(): pl.pallas_call(functools.partial(attend_back_kernel, plan), out_shape=(ja...  17.7 us
  transfers between devices with their start and end apart: 9, of which 1 were waited for; matrix products, arithmetic and copies ran while one was open for 13% of the time, Pallas kernels for 35%

profile of v2, /device:TPU:0, one launch (start us, length us, event | category | flops | bytes accessed | tf_op | source)
XLA Modules:
  0.0 520.3 jit_solution(9695285883367174023)
XLA Ops:
  8.7 4.1 collective-permute-start
  12.8 1.7 dynamic-slice_bitcast_fusion.2
  15.6 1.7 fusion.13
  17.3 2.9 collective-permute-start.3
  21.8 3.2 concatenate.74
  26.3 3.1 maximum_bitcast_fusion
  29.5 2.2 reshape.465.win
  32.4 67.6 %spread.1 = (bf16[8,128,768]{2,1,0:T(8,128)(2,1)}, bf16[32,24,640]{2,1,0:T(8,128)(2,1)}, bf16[16,24,1280]{2,1,0:T(8,128)(2,1)}) custom-call(bf16[2,128,768]{2,1,0:T(8,128)(2,1)} %bitcast.181, bf16[4,24,640]{2,1,0:T(8,128)(2,1)} %pad_maximum_fusion.4.wq, bf16[16,24,1280]{2,1,0:T(8,128)(2,1)} %reshape.465.win), custom_call_target="tpu_custom_call" | custom-call | tf_op jit(solution)/shard_map/spread/pallas_call | solution.py:149
  100.0 2.3 collective-permute-start.2
  107.0 12.1 %attend.1 = (bf16[1024,192]{1,0:T(8,128)(2,1)}, bf16[1024,768]{1,0:T(8,128)(2,1)}, bf16[1024,384]{1,0:T(8,128)(2,1)}, bf16[1024,192]{1,0:T(8,128)(2,1)}, f32[3,1024,1]{2,1,0:T(8,128)}) custom-call(s32[1]{0:T(128)} %bitcast.8.length_ref, bf16[1024,768]{1,0:T(8,128)(2,1)} %bitcast.154, f32[1,768]{1,0:T(1,128)} %reshape.484.gain, bf16[768,640]{1,0:T(8,128)(2,1)} %bitcast.158, ...), custom_call_target="tpu_custom_call" | custom-call | tf_op jit(solution)/shard_map/attend/pallas_call | solution.py:613
  119.0 31.2 %to_owners.1 = bf16[4,2,128,192]{3,2,1,0:T(8,128)(2,1)} custom-call(bf16[8,128,192]{2,1,0:T(8,128)(2,1)} %bitcast.180), custom_call_target="tpu_custom_call" | custom-call | tf_op jit(solution)/shard_map/to_owners/pallas_call | solution.py:230
  153.5 35.2 %gather.1.gy = bf16[16,256,768]{2,1,0:T(8,128)(2,1)} custom-call(bf16[256,768]{1,0:T(8,128)(2,1)} %bitcast_multiply_fusion.2.src), custom_call_target="tpu_custom_call" | custom-call | tf_op jit(solution)/shard_map/gather/pallas_call | solution.py:426
  191.2 3.1 maximum_select_fusion
  194.3 1.9 multiply_reduce_fusion.4
  198.6 111.8 %fused.1 = (f32[528,768]{1,0:T(8,128)}, bf16[768,1280]{1,0:T(8,128)(2,1)}, f32[640,768]{1,0:T(8,128)}) custom-call(bf16[272,768]{1,0:T(8,128)(2,1)} %fusion.8.n2x, bf16[16,256,768]{2,1,0:T(8,128)(2,1)} %gather.1.gy, bf16[768,1280]{1,0:T(8,128)(2,1)} %bitcast.156, bf16[640,768]{1,0:T(8,128)(2,1)} %bitcast.163, bf16[16,640]{1,0:T(8,128)(2,1)} %constant.90.clone.pick), custom_call_target="tpu_custom_call" | custom-call | tf_op jit(solution)/shard_map/fused/pallas_call | solution.py:987
  311.4 1.8 multiply_reduce_fusion.1
  314.4 2.5 collective-permute-start.7
  318.4 1.5 convolution_convert_fusion
  321.8 18.9 %to_slots.1 = bf16[8,128,192]{2,1,0:T(8,128)(2,1)} custom-call(bf16[4,2,128,192]{3,2,1,0:T(8,128)(2,1)} %bitcast.171), custom_call_target="tpu_custom_call" | custom-call | tf_op jit(solution)/shard_map/to_slots/pallas_call | solution.py:193
  340.8 2.2 dynamic-slice_bitcast_fusion
  343.0 17.7 %attend_back.1 = (bf16[1024,768]{1,0:T(8,128)(2,1)}, f32[768,640]{1,0:T(8,128)}, f32[1,768]{1,0:T(1,128)}) custom-call(s32[1]{0:T(128)} %bitcast.8.length_ref, bf16[1024,768]{1,0:T(8,128)(2,1)} %bitcast.155, bf16[768,640]{1,0:T(8,128)(2,1)} %bitcast.161, f32[1024,128]{1,0:T(8,128)} %constant.88.clone.cosine, f32[1024,128]{1,0:T(8,128)} %constant.89.clone.sine, ...), custom_call_target="tpu_custom_call" | custom-call | tf_op jit(solution)/shard_map/attend_back/pallas_call | solution.py:678
  361.7 1.7 slice.144
  363.3 3.0 collective-permute-start.5
  371.5 28.4 %collective-permute-done.5 = bf16[4,4,24,1280]{3,2,1,0:T(8,128)(2,1)S(1)} collective-permute-done((bf16[4,4,24,1280]{3,2,1,0:T(8,128)(2,1)}, bf16[4,4,24,1280]{3,2,1,0:T(8,128)(2,1)S(1)}, u32[]{:S(2)}, u32[]{:S(2)}) %collective-permute-start.5) | collective-permute-done | bytes 983072 | tf_op jit(solution)/shard_map/ppermute | solution.py:1111
  401.0 82.2 %collect.1 = (bf16[4,2,128,768]{3,2,1,0:T(8,128)(2,1)}, bf16[32,24,640]{2,1,0:T(8,128)(2,1)}, bf16[32,24,768]{2,1,0:T(8,128)(2,1)}, bf16[16,24,1280]{2,1,0:T(8,128)(2,1)}) custom-call(bf16[8,128,768]{2,1,0:T(8,128)(2,1)} %bitcast.174, bf16[32,24,640]{2,1,0:T(8,128)(2,1)} %pad_maximum_fusion.dwq, bf16[32,24,768]{2,1,0:T(8,128)(2,1)} %bitcast.162, ...), custom_call_target="tpu_custom_call" | custom-call | tf_op jit(solution)/shard_map/collect/pallas_call | solution.py:281
  483.2 1.5 convert_reduce_fusion.2
  486.6 1.7 collective-permute-start.6
  488.3 5.2 %reshape.492 = f32[4,4,24,2,5,2,64]{6,5,4,3,2,1,0:T(2,128)} reshape(bf16[16,24,1280]{2,1,0:T(8,128)(2,1)} %get-tuple-element.45) | data formatting | bytes 2949120 | tf_op jit(solution)/shard_map/convert_element_type | solution.py:1082
  493.6 6.5 %copy.164 = f32[4,4,24,2,5,2,64]{6,1,5,0,3,2,4:T(4,128)} copy(f32[4,4,24,2,5,2,64]{6,5,4,3,2,1,0:T(2,128)} %reshape.492) | data formatting | bytes 3932160 | tf_op jit(solution)/shard_map/convert_element_type | solution.py:1082
  500.1 4.1 reshape.491
  508.2 2.2 copy.142
  511.2 1.8 maximum_select_fusion.3
  (134 shorter events, 38.2 us)
Async XLA Ops:
  7.2 96.4 %copy-start = (s32[2,1]{0,1:T(1,128)S(1)}, s32[2,1]{0,1:T(1,128)}, u32[]{:S(2)}) copy-start(s32[2,1]{0,1:T(1,128)} %param.17) | copy-start | bytes 28
  7.2 13.0 %copy-start.11 = (bf16[24,2304]{1,0:T(8,128)(2,1)S(1)}, bf16[24,2304]{1,0:T(8,128)(2,1)}, u32[]{:S(2)}) copy-start(bf16[24,2304]{1,0:T(8,128)(2,1)} %param.21) | copy-start | bytes 331780
  7.2 187.1 %all-gather.2.cloned.1.call-start = ((), (), s32[]{:S(2)}) async-start(), calls=%async_computation | async-start | bytes 1216512 | tf_op jit(solution)/shard_map/all_gather | solution.py:1126
  8.7 11.9 %copy-start.12 = (bf16[24,4]{0,1:T(4,128)(2,1)S(1)}, bf16[24,4]{0,1:T(4,128)(2,1)}, u32[]{:S(2)}) copy-start(bf16[24,4]{0,1:T(4,128)(2,1)} %param.24) | copy-start | bytes 580
  8.7 11.9 %copy-start.13 = (bf16[24]{0:T(256)(128)(2,1)S(1)}, bf16[24]{0:T(256)(128)(2,1)}, u32[]{:S(2)}) copy-start(bf16[24]{0:T(256)(128)(2,1)} %param.23) | copy-start | bytes 148
  8.7 11.9 %copy-start.14 = (bf16[24]{0:T(256)(128)(2,1)S(1)}, bf16[24]{0:T(256)(128)(2,1)}, u32[]{:S(2)}) copy-start(bf16[24]{0:T(256)(128)(2,1)} %param.20) | copy-start | bytes 148
  8.7 142.9 %collective-permute-start = (s32[128,2]{0,1:T(2,128)S(1)}, s32[128,2]{0,1:T(2,128)S(1)}, u32[]{:S(2)}, u32[]{:S(2)}) collective-permute-start(s32[128,2]{0,1:T(2,128)S(1)} %get-tuple-element.114), channel_id=1, source_target_pairs={{0,4},{1,5},{2,6},{3,7},{4,0},{5,1},{6,2},{7,3},{8,12},{9,13},{10,... | collective-permute-start | bytes 3080 | tf_op jit(solution)/shard_map/ppermute | solution.py:1111
  14.5 6.6 %copy-start.10 = (bf16[24,4096]{1,0:T(8,128)(2,1)S(1)}, bf16[24,4096]{1,0:T(8,128)(2,1)}, u32[]{:S(2)}) copy-start(bf16[24,4096]{1,0:T(8,128)(2,1)} %param.25) | copy-start | bytes 589828
  14.5 137.1 %collective-permute-start.1 = (bf16[128,768]{1,0:T(8,128)(2,1)}, bf16[128,768]{1,0:T(8,128)(2,1)}, u32[]{:S(2)}, u32[]{:S(2)}) collective-permute-start(bf16[128,768]{1,0:T(8,128)(2,1)} %get-tuple-element.112), channel_id=1, source_target_pairs={{0,4},{1,5},{2,6},{3,7},{4,0},{5,1},{6,2},{7,3},{8,12},{9,13},{10,... | collective-permute-start | bytes 589832 | tf_op jit(solution)/shard_map/ppermute | solution.py:1111
  17.3 171.3 %collective-permute-start.3 = (bf16[5,64,768]{2,1,0:T(8,128)(2,1)}, bf16[5,64,768]{2,1,0:T(8,128)(2,1)}, u32[]{:S(2)}, u32[]{:S(2)}) collective-permute-start(bf16[5,64,768]{2,1,0:T(8,128)(2,1)} %get-tuple-element.106), channel_id=1, source_target_pairs={{0,4},{1,5},{2,6},{3,7},{4,0},{5,1},{6,2},{7,3},{8,12},{9,13},{10,... | collective-permute-start | bytes 1474568 | tf_op jit(solution)/shard_map/ppermute | solution.py:1111
  100.0 91.1 %collective-permute-start.2 = (bf16[16,24,1280]{2,1,0:T(8,128)(2,1)}, bf16[16,24,1280]{2,1,0:T(8,128)(2,1)}, u32[]{:S(2)}, u32[]{:S(2)}) collective-permute-start(bf16[16,24,1280]{2,1,0:T(8,128)(2,1)} %get-tuple-element.32), channel_id=1, source_target_pairs={{0,4},{1,5},{2,6},{3,7},{4,0},{5,1},{6,2},{7,3},{8,12},{9,13},{10,... | collective-permute-start | bytes 2949128 | tf_op jit(solution)/shard_map/ppermute | solution.py:1111
  188.6 2.5 copy-start.9
  314.4 53.7 %collective-permute-start.7 = (bf16[5,64,768]{2,1,0:T(8,128)(2,1)S(1)}, bf16[5,64,768]{2,1,0:T(8,128)(2,1)}, u32[]{:S(2)}, u32[]{:S(2)}) collective-permute-start(bf16[5,64,768]{2,1,0:T(8,128)(2,1)S(1)} %fusion.7), channel_id=1, source_target_pairs={{0,4},{1,5},{2,6},{3,7},{4,0},{5,1},{6,2},{7,3},{8,12},{9,13},{10,... | collective-permute-start | bytes 1474568 | tf_op jit(solution)/shard_map/ppermute | solution.py:1111
  318.4 1.6 copy-start.3
  340.7 26.7 %collective-permute-start.4 = (bf16[128,768]{1,0:T(8,128)(2,1)S(1)}, bf16[128,768]{1,0:T(8,128)(2,1)S(1)}, u32[]{:S(2)}, u32[]{:S(2)}) collective-permute-start(bf16[128,768]{1,0:T(8,128)(2,1)S(1)} %get-tuple-element.110), channel_id=1, source_target_pairs={{0,4},{1,5},{2,6},{3,7},{4,0},{5,1},{6,2},{7,3},{8,12},{9,13},{10,... | collective-permute-start | bytes 589832 | tf_op jit(solution)/shard_map/ppermute | solution.py:1111
  363.3 4.9 copy-start.8
  363.3 36.5 %collective-permute-start.5 = (bf16[4,4,24,1280]{3,2,1,0:T(8,128)(2,1)}, bf16[4,4,24,1280]{3,2,1,0:T(8,128)(2,1)S(1)}, u32[]{:S(2)}, u32[]{:S(2)}) collective-permute-start(bf16[4,4,24,1280]{3,2,1,0:T(8,128)(2,1)} %dynamic-slice_bitcast_fusion), channel_id=1, source_target_pairs={{0,4},{1,5},{2,6},{3,7},{4,0},{5,1},{6,2},{7,3},{8,12},{9,13},{10,... | collective-permute-start | bytes 2949128 | tf_op jit(solution)/shard_map/ppermute | solution.py:1111
  369.3 30.5 %copy-start.4 = (bf16[768,1280]{1,0:T(8,128)(2,1)S(1)}, bf16[768,1280]{1,0:T(8,128)(2,1)}, u32[]{:S(2)}) copy-start(bf16[768,1280]{1,0:T(8,128)(2,1)} %get-tuple-element.41) | copy-start | bytes 5898244
  483.2 1.7 copy-start.5
  484.6 0.7 copy-start.6
  485.3 0.9 slice-start.1
  485.4 1.0 slice-start.2
  486.6 24.6 %collective-permute-start.6 = (bf16[128,768]{1,0:T(8,128)(2,1)S(1)}, bf16[128,768]{1,0:T(8,128)(2,1)}, u32[]{:S(2)}, u32[]{:S(2)}) collective-permute-start(bf16[128,768]{1,0:T(8,128)(2,1)S(1)} %get-tuple-element.108), channel_id=1, source_target_pairs={{0,4},{1,5},{2,6},{3,7},{4,0},{5,1},{6,2},{7,3},{8,12},{9,13},{10,... | collective-permute-start | bytes 589832 | tf_op jit(solution)/shard_map/ppermute | solution.py:1111
  504.2 1.9 copy-start.2
  506.8 1.4 slice-start
  507.0 6.0 %copy-start.1 = (s32[2,1]{0,1:T(1,128)S(1)}, s32[2,1]{0,1:T(1,128)}, u32[]{:S(2)}) copy-start(s32[2,1]{0,1:T(1,128)} %param.17) | copy-start | bytes 28
  508.2 2.2 copy-start.7
Sparse Core Ops, SparseCore 0:
  11.0 73.9 all-gather.1
